TPU v7x, 128 devices: a whole 4x4x4 slice. The times are simulated.
128 devices in a mesh: stn: 64 (over z, y, x_hi, core), tm: 2 (over x_lo).
Axes of the slice: x: 4 (x_hi: 2, x_lo: 2; x = x_hi * 2 + x_lo), y: 4, z: 4, core: 2. Of those that a mesh axis runs over, the one named last changes fastest.
Arguments:
- voltages: bfloat16 [2, 1024, 131072], P(None, 'stn', 'tm'), may hold values from -6 to 6
- filter_taps: float32 [16, 4096], replicated, may hold values from -1.5 to 1.5
- membership: int32 [128, 512], P('stn'), may hold values from 0 to 3
- block_active: int32 [128, 10], P('stn'), may hold values 0 or 1
Outputs:
- visibilities: float32 [128, 10, 2, 256, 256], P('stn', None, None, 'tm')
All inputs are finite; a program needn't handle non-finite values. No bound on the sum of `block_active` on one device may be relied on, other than what follows from the above.
Results may differ from a plain program's by a relative error of at most 0.006.
Values may be sent and summed in bfloat16 or wider, within the bound.
No kernel may reach another device: no remote copies, remote signals or barrier semaphores. Data moves between devices by JAX's collectives and lax.ppermute only.
A program may use at most 128 MiB of HBM per device.

v0:
```python
import math

import jax
import jax.numpy as jnp
import numpy as np
from jax import lax
from jax.sharding import PartitionSpec as P

TAPS = 16
RADIX = 64
FFT = 4096
AVG = 16
CH_DEV = 2
F_DEV = 16


def passed_along(shard, axis, by):
    devices = lax.axis_size(axis)
    pairs = [(i, i + by) for i in range(devices) if 0 <= i + by < devices]
    return lax.ppermute(shard, axis, pairs)


def pair_tables(count):
    upper_list = []
    lower_list = []
    for upper in range(count):
        for lower in range(upper + 1):
            upper_list.append(upper)
            lower_list.append(lower)
    return (np.array(upper_list, dtype=np.int32), np.array(lower_list, dtype=np.int32))


def rotation(numer, denom):
    angle = -2.0 * math.pi * numer.astype(jnp.float32) / denom
    return (jnp.cos(angle), jnp.sin(angle))


def complex_table(cosine, sine):
    upper_rows = jnp.stack([cosine, sine], axis=1)
    lower_rows = jnp.stack([-sine, cosine], axis=1)
    return jnp.stack([upper_rows, lower_rows])


def apply_filter(padded, filter_taps, frame_count):
    filtered = filter_taps[0] * padded[:, :, 0:frame_count, :].astype(jnp.float32)
    for tap_index in range(1, TAPS):
        filtered = filtered + filter_taps[tap_index] * padded[
            :, :, tap_index : tap_index + frame_count, :
        ].astype(jnp.float32)
    return filtered


def transform(filtered):
    local_inputs = filtered.shape[1]
    frame_count = filtered.shape[2]
    frame_grid = filtered.reshape(2, local_inputs, frame_count, RADIX, RADIX)
    counter = lax.iota(jnp.int32, RADIX)
    cosine_one, sine_one = rotation(counter[:, None] * counter[None, :] % RADIX, RADIX)
    section_one = jnp.einsum(
        "cifab,cadk->difbk",
        frame_grid,
        complex_table(cosine_one, sine_one),
        precision=lax.Precision.HIGHEST,
    )
    cosine_two, sine_two = rotation(counter[:, None] * counter[None, :], FFT)
    turned = jnp.stack(
        [
            section_one[0] * cosine_two - section_one[1] * sine_two,
            section_one[0] * sine_two + section_one[1] * cosine_two,
        ]
    )
    station_devices = lax.axis_size("stn")
    per_device = CH_DEV * AVG
    pick_count = station_devices * per_device // RADIX
    chosen = (lax.iota(jnp.int32, pick_count) - pick_count // 2) % RADIX
    cosine_three, sine_three = rotation(counter[:, None] * chosen[None, :] % RADIX, RADIX)
    second_table = complex_table(cosine_three, sine_three) / RADIX
    shaped = turned.reshape(2, local_inputs, frame_count, RADIX, RADIX // per_device, per_device)
    return jnp.einsum("cifbhl,cbdj->dijhfl", shaped, second_table, precision=lax.Precision.HIGHEST)


def channelize(voltages, filter_taps):
    local_inputs = voltages.shape[1]
    station_devices = lax.axis_size("stn")
    per_device = CH_DEV * AVG
    own_frames = voltages.reshape(2, local_inputs, F_DEV, FFT)
    tail_frames = own_frames[:, :, F_DEV - TAPS + 1 :, :]
    history_frames = passed_along(tail_frames, "tm", 1)
    padded = jnp.concatenate([history_frames, own_frames], axis=2)
    spectrum = transform(apply_filter(padded, filter_taps, F_DEV))
    return spectrum.reshape(2, local_inputs, station_devices, F_DEV * per_device).astype(
        jnp.bfloat16
    )


def shards(voltages, filter_taps, membership, block_active):
    spectrum = channelize(voltages, filter_taps)
    gathered = lax.all_to_all(spectrum, "stn", split_axis=2, concat_axis=1, tiled=True)
    inputs_all = gathered.shape[1]
    block_size = inputs_all // 4
    upper_tab, lower_tab = pair_tables(4)
    time_devices = lax.axis_size("tm")
    scale = 1.0 / (AVG * F_DEV * time_devices)
    arranged = gathered.reshape(2, inputs_all, F_DEV, CH_DEV, AVG)
    results = []
    for channel in range(CH_DEV):
        samples = arranged[:, :, :, channel, :].reshape(2, inputs_all, F_DEV * AVG)
        left = jnp.concatenate([samples[0], samples[1]], axis=1)
        swapped = jnp.concatenate([samples[1], -samples[0]], axis=1)
        both_sides = jnp.stack([left, swapped])
        flags = block_active[channel]
        rows_left = both_sides.reshape(2, 4, block_size, -1)[:, upper_tab]
        rows_right = left.reshape(4, block_size, -1)[lower_tab]
        product = jnp.einsum(
            "cpik,pjk->pcij", rows_left, rows_right, preferred_element_type=jnp.float32
        )
        station_ids = jnp.repeat(membership[channel], 2).reshape(4, block_size)
        same = (station_ids[upper_tab][:, :, None] == station_ids[lower_tab][:, None, :]).astype(
            jnp.float32
        )
        weight = same * flags.astype(jnp.float32)[:, None, None]
        results.append(product * scale * weight[:, None])
    partial_value = jnp.stack(results)
    summed = lax.psum(partial_value.astype(jnp.bfloat16), "tm").astype(jnp.float32)
    share = block_size // time_devices
    return lax.dynamic_slice_in_dim(summed, lax.axis_index("tm") * share, share, 3)


def solution(mesh):
    placed = (P(None, "stn", "tm"), P(), P("stn", None), P("stn", None))
    return jax.shard_map(
        shards,
        mesh=mesh,
        in_specs=placed,
        out_specs=P("stn", None, None, "tm", None),
        check_vma=False,
    )
```

profile of v0, /device:TPU:1, one launch (start us, length us, event | category | flops | bytes accessed | tf_op | source)
XLA Modules:
  0.0 531.1 jit_solution(13981688609967361830)
XLA Ops:
  6.5 4.5 copy.124
  12.4 2.3 copy.90
  14.8 4.2 collective-permute-start
  19.8 82.5 %collective-permute-done = bf16[2,16,15,4096]{3,1,2,0:T(8,128)(2,1)S(1)} collective-permute-done((bf16[2,16,15,4096]{3,1,2,0:T(8,128)(2,1)S(1)}, bf16[2,16,15,4096]{3,1,2,0:T(8,128)(2,1)S(1)}, u32[]{:S(2)}, u32[]{:S(2)}) %collective-permute-start) | collective-permute-done | bytes 3932192 | tf_op jit(solution)/shard_map/ppermute | solution.py:20
  104.5 25.7 %multiply_add_fusion.1 = f32[2,16,16,4096]{3,2,1,0:T(8,128)} fusion(bf16[2,16,16,4096]{3,2,1,0:T(8,128)(2,1)S(1)} %bitcast.152, bf16[2,16,15,4096]{3,2,1,0:T(8,128)(2,1)S(1)} %copy.91, f32[4096]{0:T(1024)S(1)} %bitcast.175, f32[4096]{0:T(1024)S(1)} %bitcast.176, f32[4096]{0:T(1024)S(1)} %bitcast.162, f32[4096]{0:T(1024)S(1)} %bitcast.163, ...), kind=kLoop, calls=%fused_computation.47 | loop fusion | flops 192937984 | bytes 16777216 | tf_op jit(solution)/shard_map/add | solution.py:47
  130.2 14.2 %reshape.346 = f32[2,16,16,64,64]{4,3,2,1,0:T(8,128)} reshape(f32[2,16,16,4096]{3,2,1,0:T(8,128)} %multiply_add_fusion.1) | data formatting | bytes 16777216 | tf_op jit(solution)/shard_map/reshape | solution.py:56
  144.3 22.3 %fusion.7 = f32[2,16,16,64,64]{3,4,2,1,0:T(8,128)} fusion(f32[2,16,16,64,64]{4,3,2,1,0:T(8,128)} %reshape.346, f32[1,64,2,64]{1,3,0,2:T(8,128)S(1)} %get-tuple-element.28, f32[1,64,2,64]{1,3,0,2:T(8,128)S(1)} %get-tuple-element.27), kind=kOutput, calls=%fused_computation.48 | convolution fusion | flops 3221241856 | bytes 16842752 | tf_op jit(solution)/shard_map/cifab,cadk->difbk/dot_general | solution.py:59
  166.6 7.2 %multiply_subtract_fusion = (f32[1,16,16,64,64]{3,4,2,1,0:T(8,128)S(1)}, f32[1,16,16,64,64]{3,4,2,1,0:T(8,128)S(1)}) fusion(f32[2,16,16,64,64]{3,4,2,1,0:T(8,128)} %fusion.7, f32[64,64]{0,1:T(8,128)S(1)} %get-tuple-element.40, f32[64,64]{0,1:T(8,128)S(1)} %get-tuple-element.41), kind=kLoop, calls=%fused_computation.46 | loop fusion | flops 6291456 | bytes 16809984 | tf_op jit(solution)/shard_map/sub | solution.py:68
  173.8 43.7 %fusion.6 = bf16[2,16,32,2,16,32]{5,2,3,4,1,0:T(8,128)(2,1)} fusion(f32[1,16,16,64,2,32]{3,5,0,4,2,1:T(8,128)S(1)} %bitcast.154, f32[1,16,16,64,2,32]{3,5,0,4,2,1:T(8,128)S(1)} %bitcast.153, f32[1,64,2,32]{1,3,0,2:T(8,128)S(1)} %get-tuple-element.30, f32[1,64,2,32]{1,3,0,2:T(8,128)S(1)} %get-tuple-element.29), kind=kOutput, calls=%fused_computation.44 | convolution fusion | flops 1613774848 | bytes 10518528 | tf_op jit(solution)/shard_map/cifbhl,cbdj->dijhfl/dot_general | solution.py:79
  217.6 12.0 %copy.122 = bf16[2,16,32,2,16,32]{5,4,1,0,3,2:T(8,128)(2,1)} copy(bf16[2,16,32,2,16,32]{5,2,3,4,1,0:T(8,128)(2,1)} %fusion.6) | data formatting | bytes 4194304 | tf_op jit(solution)/shard_map/convert_element_type | solution.py:91
  229.6 12.0 %reshape.420 = bf16[2,16,64,512]{3,1,0,2:T(8,128)(2,1)} reshape(bf16[2,16,32,2,16,32]{5,4,1,0,3,2:T(8,128)(2,1)} %copy.122) | data formatting | bytes 4194304 | tf_op jit(solution)/shard_map/convert_element_type | solution.py:91
  241.6 12.2 %all-to-all-start = ((bf16[2,16,64,512]{3,1,0,2:T(8,128)(2,1)}), bf16[2,16,64,512]{3,1,0,2:T(8,128)(2,1)S(1)}, u32[]{:S(2)}, u32[]{:S(2)}) async-start(bf16[2,16,64,512]{3,1,0,2:T(8,128)(2,1)} %reshape.420), calls=%async_computation | async-start | bytes 4194304 | tf_op jit(solution)/shard_map/all_to_all | solution.py:98
  256.7 3.3 select_multiply_fusion
  260.0 24.9 %all-to-all-done = bf16[2,16,64,512]{3,1,0,2:T(8,128)(2,1)S(1)} async-done(((bf16[2,16,64,512]{3,1,0,2:T(8,128)(2,1)}), bf16[2,16,64,512]{3,1,0,2:T(8,128)(2,1)S(1)}, u32[]{:S(2)}, u32[]{:S(2)}) %all-to-all-start) | async-done | bytes 2097184 | tf_op jit(solution)/shard_map/all_to_all | solution.py:98
  284.9 22.9 %copy.97 = bf16[2,64,16,1,512]{2,1,4,0,3:T(8,128)(2,1)} copy(bf16[2,64,16,1,512]{4,2,0,1,3:T(8,128)(2,1)S(1)} %bitcast.157) | data formatting | bytes 4194304 | tf_op jit(solution)/shard_map/all_to_all | solution.py:98
  307.8 29.1 %reshape.347 = bf16[2,1024,16,2,16]{1,4,3,2,0:T(8,128)(2,1)S(1)} reshape(bf16[2,64,16,1,512]{2,1,4,0,3:T(8,128)(2,1)} %copy.97) | data formatting | bytes 4194304 | tf_op jit(solution)/shard_map/reshape | solution.py:104
  353.2 3.8 gather_fusion
  359.9 2.4 gather_fusion.1
  365.2 4.0 gather_fusion.4
  372.0 2.5 gather_fusion.5
  374.4 5.7 %fusion.28 = bf16[1,10,2,256,256]{4,3,2,1,0:T(8,128)(2,1)S(1)} fusion(f32[10,256,256]{2,1,0:T(8,128)} %get-tuple-element.43, bf16[10,256,512]{2,1,0:T(8,128)(2,1)} %gather_fusion.1, bf16[10,2,256,512]{3,2,1,0:T(8,128)(2,1)} %gather_fusion), kind=kOutput, calls=%fused_computation.71 | convolution fusion | flops 1344798720 | bytes 13107200 | tf_op jit(solution)/shard_map/cpik,pjk->pcij/dot_general | solution.py:114
  382.9 2.8 pad_maximum_fusion
  385.7 133.5 %all-reduce.2.cloned.1.call-done = bf16[2,10,2,256,256]{4,3,2,1,0:T(8,128)(2,1)} async-done(((bf16[2,10,2,256,256]{4,3,2,1,0:T(8,128)(2,1)}), bf16[2,10,2,256,256]{4,3,2,1,0:T(8,128)(2,1)}) %all-reduce.2.cloned.1.call-update) | async-done | bytes 5242896 | tf_op jit(solution)/shard_map/psum | solution.py:124
  519.3 4.8 dynamic-slice_convert_fusion
  (73 shorter events, 34.7 us)
Async XLA Ops:
  11.1 8.5 %copy-start.4 = (f32[16,4096]{1,0:T(8,128)S(1)}, f32[16,4096]{1,0:T(8,128)}, u32[]{:S(2)}) copy-start(f32[16,4096]{1,0:T(8,128)} %param.15) | copy-start | bytes 786436
  14.8 87.6 %collective-permute-start = (bf16[2,16,15,4096]{3,1,2,0:T(8,128)(2,1)S(1)}, bf16[2,16,15,4096]{3,1,2,0:T(8,128)(2,1)S(1)}, u32[]{:S(2)}, u32[]{:S(2)}) collective-permute-start(bf16[2,16,15,4096]{3,1,2,0:T(8,128)(2,1)S(1)} %copy.90), channel_id=1, source_target_pairs={{0,1},{2,3},{4,5},{6,7},{8,9},{10,11},{12,13},{14,15},{16,17},{18,... | collective-permute-start | bytes 11796488 | tf_op jit(solution)/shard_map/ppermute | solution.py:20
  229.5 24.3 %copy-start.5 = (s32[2,512]{1,0:T(2,128)S(1)}, s32[2,512]{1,0:T(2,128)}, u32[]{:S(2)}) copy-start(s32[2,512]{1,0:T(2,128)} %param.16) | copy-start | bytes 12292
  229.5 24.6 %copy-start.7 = (s32[10]{0:T(128)S(1)}, s32[10]{0:T(128)}, u32[]{:S(2)}) copy-start(s32[10]{0:T(128)} %constant.80) | copy-start | bytes 124
  229.5 25.2 %copy-start.8 = (s32[10]{0:T(128)S(1)}, s32[10]{0:T(128)}, u32[]{:S(2)}) copy-start(s32[10]{0:T(128)} %constant.81) | copy-start | bytes 124
  229.6 27.1 %copy-start.6 = (s32[2,10]{1,0:T(2,128)S(1)}, s32[2,10]{1,0:T(2,128)}, u32[]{:S(2)}) copy-start(s32[2,10]{1,0:T(2,128)} %param.17) | copy-start | bytes 244
  241.6 43.3 %all-to-all-start = ((bf16[2,16,64,512]{3,1,0,2:T(8,128)(2,1)}), bf16[2,16,64,512]{3,1,0,2:T(8,128)(2,1)S(1)}, u32[]{:S(2)}, u32[]{:S(2)}) async-start(bf16[2,16,64,512]{3,1,0,2:T(8,128)(2,1)} %reshape.420), calls=%async_computation | async-start | bytes 4194304 | tf_op jit(solution)/shard_map/all_to_all | solution.py:98
  253.8 265.5 %all-reduce.2.cloned.1.call-start = ((), (), s32[]{:S(2)}) async-start(), calls=%async_computation.1 | async-start | bytes 10485760 | tf_op jit(solution)/shard_map/psum | solution.py:124
  353.2 9.0 %copy-start.2 = (bf16[1,4,256,256]{2,1,3,0:T(4,128)(2,1)S(1)}, bf16[1,4,256,256]{2,1,3,0:T(4,128)(2,1)}, u32[]{:S(2)}) copy-start(bf16[1,4,256,256]{2,1,3,0:T(4,128)(2,1)} %concatenate.52) | copy-start | bytes 1572868
  357.1 5.6 %copy-start.3 = (bf16[1,4,256,256]{2,1,3,0:T(4,128)(2,1)S(1)}, bf16[1,4,256,256]{2,1,3,0:T(4,128)(2,1)}, u32[]{:S(2)}) copy-start(bf16[1,4,256,256]{2,1,3,0:T(4,128)(2,1)} %concatenate.53) | copy-start | bytes 1572868
  372.0 8.2 %slice-start = ((s8[5242880]{0:T(1024)(128)(4,1)}), s8[1048576]{0:T(1024)(128)(4,1)S(1)}, s32[]{:S(2)}) async-start(s8[5242880]{0:T(1024)(128)(4,1)} %bitcast.155), calls=%async_computation.2 | async-start | bytes 2097152
  374.4 5.8 %copy-start = (f32[10,256,256]{2,1,0:T(8,128)S(1)}, f32[10,256,256]{2,1,0:T(8,128)}, u32[]{:S(2)}) copy-start(f32[10,256,256]{2,1,0:T(8,128)} %get-tuple-element.42) | copy-start | bytes 7864324
  374.4 5.8 %copy-start.1 = (bf16[10,256,512]{2,1,0:T(8,128)(2,1)S(1)}, bf16[10,256,512]{2,1,0:T(8,128)(2,1)}, u32[]{:S(2)}) copy-start(bf16[10,256,512]{2,1,0:T(8,128)(2,1)} %gather_fusion.5) | copy-start | bytes 7864324
  374.4 6.8 %slice-start.1 = ((s8[5242880]{0:T(1024)(128)(4,1)}), s8[4194304]{0:T(1024)(128)(4,1)S(1)}, s32[]{:S(2)}) async-start(s8[5242880]{0:T(1024)(128)(4,1)} %bitcast.155), calls=%async_computation.3 | async-start | bytes 8388608
Sparse Core Ops, SparseCore 0:
  385.9 133.3 all-reduce.1
where the time goes:
time: 540 us; the launch traced here: 531 us
  waiting for transfers between devices  241 us (45%)
  local copies, waits for them, and re-layouts  139 us (26%)
  matrix products  73.4 us (14%)
  other arithmetic  47.6 us (9%)
  starting transfers between devices  16.4 us (3%)
  between operations  14 us (3%)
    psum x1, waiting for transfers between devices, shards(): lax.psum(partial_value.astype(jnp.bfloat16), 'tm').astype(jnp.float32)  134 us
    ppermute x1, waiting for transfers between devices, passed_along(): return lax.ppermute(shard, axis, pairs)  82.5 us
    dot_general x1, matrix products, transform(): jnp.einsum('cifbhl,cbdj->dijhfl', shaped, second_table, precision=lax.Pre...  43.7 us
    reshape x1, local copies, waits for them, and re-layouts, shards(): arranged = gathered.reshape(2, inputs_all, F_DEV, CH_DEV, AVG)  29.1 us
    add x1, other arithmetic, apply_filter(): filtered + filter_taps[tap_index] * padded[:, :, tap_index:tap_index + fr...  25.7 us
    all_to_all x1, waiting for transfers between devices, shards(): lax.all_to_all(spectrum, 'stn', split_axis=2, concat_axis=1, tiled=True)  24.9 us
    convert_element_type x2, local copies, waits for them, and re-layouts, channelize(): spectrum.reshape(2, local_inputs, station_devices, F_DEV * per_device)  24 us
    all_to_all x1, local copies, waits for them, and re-layouts, shards(): lax.all_to_all(spectrum, 'stn', split_axis=2, concat_axis=1, tiled=True)  22.9 us
  transfers between devices with their start and end apart: 3, of which 3 were waited for; matrix products, arithmetic and copies ran while one was open for 1% of the time, Pallas kernels for 0%

commit v1 on v0

v1 whole, which is shorter than its diff:
```python
import functools
import math

import jax
import jax.numpy as jnp
import numpy as np
from jax import lax
from jax.experimental import pallas as pl
from jax.experimental.pallas import tpu as pltpu
from jax.sharding import PartitionSpec as P

TAPS = 16
FFT = 4096
LANES = 128
ROWS = FFT // LANES
AVG = 16
F_DEV = 16
PAIRS = ((0, 0), (1, 0), (1, 1), (2, 0), (2, 1), (2, 2), (3, 0), (3, 1), (3, 2), (3, 3))
PART = 8


def tables():
    q = np.arange(ROWS)
    l = np.arange(LANES)
    angle = 2 * np.pi * np.outer(q, q) / ROWS
    one = np.block([[np.cos(angle), np.sin(angle)], [-np.sin(angle), np.cos(angle)]])
    angle = 2 * np.pi * np.outer(q, l) / FFT
    turn = np.stack([np.cos(angle), -np.sin(angle)])
    angle = 2 * np.pi * np.outer(np.arange(64) - 32, l) / LANES
    two = np.block([[np.cos(angle), np.sin(angle)], [-np.sin(angle), np.cos(angle)]]) / 64
    bf = jnp.bfloat16
    return jnp.asarray(one, bf), jnp.asarray(turn, jnp.float32), jnp.asarray(two, bf)


def spectra_kernel(tail, x_ref, taps_ref, one_ref, turn_ref, two_ref, out_ref, fir, mid, spread):
    def one_input(i, carry):
        for c in range(2):
            for q in range(0, ROWS, 8):
                x = [x_ref[c, i, m, q : q + 8, :].astype(jnp.float32) for m in range(F_DEV)]
                w = [taps_ref[t, q : q + 8, :] for t in range(TAPS)]
                for m in range(F_DEV):
                    total = None
                    for t in range(TAPS):
                        frame = m - (TAPS - 1) + t + (F_DEV if tail else 0)
                        if 0 <= frame < F_DEV:
                            term = w[t] * x[frame]
                            total = term if total is None else total + term
                    if total is None:
                        total = jnp.zeros((8, LANES), jnp.float32)
                    fir[c * ROWS + q : c * ROWS + q + 8, m * LANES : (m + 1) * LANES] = total
        for m in range(0, F_DEV, 2):
            first = jnp.dot(
                one_ref[...],
                fir[:, m * LANES : (m + 2) * LANES].astype(jnp.bfloat16),
                preferred_element_type=jnp.float32,
            )
            for k in range(2):
                re = first[:ROWS, k * LANES : (k + 1) * LANES]
                im = first[ROWS:, k * LANES : (k + 1) * LANES]
                parts = (
                    re * turn_ref[0] - im * turn_ref[1],
                    re * turn_ref[1] + im * turn_ref[0],
                )
                for c in range(2):
                    value = parts[c].astype(jnp.bfloat16)
                    for h in range(2):
                        row = h * 256 + (m + k) * AVG
                        mid[row : row + AVG, c * LANES : (c + 1) * LANES] = value[
                            h * AVG : (h + 1) * AVG
                        ]
        for h in range(2):
            second = lax.dot_general(
                two_ref[...],
                mid[h * 256 : (h + 1) * 256, :],
                (((1,), (1,)), ((), ())),
                preferred_element_type=jnp.float32,
            )
            for c in range(2):
                for b in range(2):
                    for j in range(0, 64, 8):
                        spread[h, c, b, pl.ds(j * PART + i, 8, stride=PART), :] = second[
                            c * 64 + j : c * 64 + j + 8, b * LANES : (b + 1) * LANES
                        ]
        return carry

    lax.fori_loop(0, PART, one_input, 0)
    for h in range(2):
        for c in range(2):
            for b in range(2):
                start = c * 256 + b * LANES
                out_ref[:, h, :, start : start + LANES] = (
                    spread[h, c, b].reshape(64, PART, LANES).astype(jnp.bfloat16)
                )


def spectra(x, taps, consts, tail):
    inputs = x.shape[1]
    one, turn, two = consts
    whole = lambda a: pl.BlockSpec(a.shape, lambda g: (0,) * a.ndim)
    return pl.pallas_call(
        functools.partial(spectra_kernel, tail),
        grid=(inputs // PART,),
        in_specs=[
            pl.BlockSpec((2, PART, F_DEV, ROWS, LANES), lambda g: (0, g, 0, 0, 0)),
            whole(taps),
            whole(one),
            whole(turn),
            whole(two),
        ],
        out_specs=pl.BlockSpec((64, 2, PART, 512), lambda g: (0, 0, g, 0)),
        out_shape=jax.ShapeDtypeStruct((64, 2, inputs, 512), jnp.bfloat16),
        scratch_shapes=[
            pltpu.VMEM((2 * ROWS, F_DEV * LANES), jnp.float32),
            pltpu.VMEM((512, 256), jnp.bfloat16),
            pltpu.VMEM((2, 2, 2, 64 * PART, LANES), jnp.float32),
        ],
        compiler_params=pltpu.CompilerParams(vmem_limit_bytes=48 << 20),
        cost_estimate=pl.CostEstimate(
            flops=4 * 10**9, bytes_accessed=8 << 20, transcendentals=0
        ),
        name="tail" if tail else "head",
    )(x, taps, one, turn, two)


def gram_kernel(info, main_ref, tail_ref, row_ref, col_ref, out_ref, send_ref, left, turned):
    p = pl.program_id(0)

    @pl.when(p == 0)
    def _():
        for t in range(2):
            value = main_ref[:, t]
            if t:
                value = (value.astype(jnp.float32) + tail_ref[:, 0].astype(jnp.float32)).astype(
                    jnp.bfloat16
                )
            value = value.reshape(1024, 512)
            left[:, t * 512 : (t + 1) * 512] = value
            turned[:, t * 512 : t * 512 + 256] = value[:, 256:]
            turned[:, t * 512 + 256 : (t + 1) * 512] = -value[:, :256]

    upper = (p >= 1).astype(jnp.int32) + (p >= 3).astype(jnp.int32) + (p >= 6).astype(jnp.int32)
    lower = p - upper * (upper + 1) // 2
    mine = info[0]
    flag = info[1 + p].astype(jnp.float32) * (1.0 / 512)
    cols = pl.ds(pl.multiple_of(lower * 256, 256), 256)
    right = left[cols, :]
    ids = row_ref[lower]
    for other in range(2):
        half = (1 - mine) if other else mine
        rows = pl.ds(pl.multiple_of(upper * 256 + half * 128, 128), 128)
        weight = jnp.where(col_ref[rows, :] == ids, flag, 0.0)
        for c, source in enumerate((left, turned)):
            product = lax.dot_general(
                source[rows, :],
                right,
                (((1,), (1,)), ((), ())),
                preferred_element_type=jnp.float32,
            )
            if other:
                send_ref[0, c] = (product * weight).astype(jnp.bfloat16)
            else:
                out_ref[0, 0, c] = product * weight


def gram(info, main, tail, row_ids, col_ids):
    stations = main.shape[0]
    return pl.pallas_call(
        gram_kernel,
        grid_spec=pltpu.PrefetchScalarGridSpec(
            num_scalar_prefetch=1,
            grid=(len(PAIRS),),
            in_specs=[
                pl.BlockSpec(main.shape, lambda p, s: (0, 0, 0, 0), pipeline_mode=pl.Buffered(1)),
                pl.BlockSpec(
                    (stations, 1) + tail.shape[2:],
                    lambda p, s: (0, 0, 0, 0),
                    pipeline_mode=pl.Buffered(1),
                ),
                pl.BlockSpec(row_ids.shape, lambda p, s: (0, 0, 0)),
                pl.BlockSpec(col_ids.shape, lambda p, s: (0, 0)),
            ],
            out_specs=[
                pl.BlockSpec((1, 1, 2, 128, 256), lambda p, s: (s[0], p, 0, 0, 0)),
                pl.BlockSpec((1, 2, 128, 256), lambda p, s: (p, 0, 0, 0)),
            ],
            scratch_shapes=[
                pltpu.VMEM((1024, 1024), jnp.bfloat16),
                pltpu.VMEM((1024, 1024), jnp.bfloat16),
            ],
        ),
        out_shape=[
            jax.ShapeDtypeStruct((2, 10, 2, 128, 256), jnp.float32),
            jax.ShapeDtypeStruct((10, 2, 128, 256), jnp.bfloat16),
        ],
        compiler_params=pltpu.CompilerParams(vmem_limit_bytes=48 << 20),
        name="gram",
    )(info, main, tail, row_ids, col_ids)


def fill_kernel(info, whole_ref, got_ref, out_ref):
    out_ref[0] = got_ref[...].astype(jnp.float32)


def fill(info, whole, got):
    return pl.pallas_call(
        fill_kernel,
        grid_spec=pltpu.PrefetchScalarGridSpec(
            num_scalar_prefetch=1,
            grid=(5,),
            in_specs=[
                pl.BlockSpec(memory_space=pl.ANY),
                pl.BlockSpec((2, 2, 128, 256), lambda p, s: (p, 0, 0, 0)),
            ],
            out_specs=pl.BlockSpec((1, 2, 2, 128, 256), lambda p, s: (1 - s[0], p, 0, 0, 0)),
        ),
        out_shape=jax.ShapeDtypeStruct(whole.shape, whole.dtype),
        input_output_aliases={1: 0},
        name="fill",
    )(info, whole, got)


def exchanged(x):
    devices = lax.axis_size("stn") * lax.axis_size("tm")
    flat = x.reshape((devices,) + x.shape[2:])
    return lax.all_to_all(flat, ("stn", "tm"), split_axis=0, concat_axis=0, tiled=True).reshape(
        x.shape
    )


def shards(voltages, filter_taps, membership, block_active):
    inputs = voltages.shape[1]
    mine = lax.axis_index("tm")
    consts = tables()
    x = voltages.reshape(2, inputs, F_DEV, ROWS, LANES)
    taps = filter_taps.reshape(TAPS, ROWS, LANES)
    main = exchanged(spectra(x, taps, consts, False))
    tail = exchanged(spectra(x, taps, consts, True))
    ids = jnp.repeat(lax.dynamic_index_in_dim(membership, mine, 0, keepdims=False), 2)
    flags = lax.dynamic_index_in_dim(block_active, mine, 0, keepdims=False)
    info = jnp.concatenate([mine.astype(jnp.int32)[None], flags])
    whole, send = gram(info, main, tail, ids.reshape(4, 1, 256), ids.reshape(1024, 1))
    got = lax.ppermute(send, "tm", [(0, 1), (1, 0)])
    return fill(info, whole, got)


def solution(mesh):
    placed = (P(None, "stn", "tm"), P(), P("stn", None), P("stn", None))
    return jax.shard_map(
        shards,
        mesh=mesh,
        in_specs=placed,
        out_specs=P("stn", None, None, "tm", None),
        check_vma=False,
    )
```

time: 540 us -> 147 us (0.27); the launches traced: 531 us -> 146 us
  waiting for transfers between devices: 241 us -> 73.3 us
  local copies, waits for them, and re-layouts: 139 us -> 10.5 us
  matrix products: 73.4 us -> 0 us
  other arithmetic: 47.6 us -> 0.08 us
  Pallas kernels: 0 us -> 44.2 us
  between operations: 14 us -> 0.14 us
    psum x1 -> x0, waiting for transfers between devices: 134 us -> none  [shards(): lax.psum(partial_value.astype(jnp.bfloat16), 'tm').astype(jnp.float32)]
    dot_general x4 -> x0, matrix products: 73.4 us -> none  [the longest x1 43.7 us: transform(): jnp.einsum('cifbhl,cbdj->dijhfl', shaped, second_table, precision=lax.Pre...]
    ppermute x1, waiting for transfers between devices: 82.5 us -> 29 us  [shards(): got = lax.ppermute(send, 'tm', [(0, 1), (1, 0)])]
    pallas_call x0 -> x4, Pallas kernels: none -> 44.2 us  [the longest x2 27.7 us: spectra(): pl.pallas_call(functools.partial(spectra_kernel, tail), grid=(inputs // P...]
    reshape x2 -> x0, local copies, waits for them, and re-layouts: 43.2 us -> none  [the longest x1 29.1 us: shards(): arranged = gathered.reshape(2, inputs_all, F_DEV, CH_DEV, AVG)]
    add x1 -> x0, other arithmetic: 25.7 us -> none  [apply_filter(): filtered + filter_taps[tap_index] * padded[:, :, tap_index:tap_index + fr...]
    convert_element_type x2 -> x0, local copies, waits for them, and re-layouts: 24 us -> none  [channelize(): spectrum.reshape(2, local_inputs, station_devices, F_DEV * per_device)]
    all_to_all x1 -> x0, local copies, waits for them, and re-layouts: 22.9 us -> none  [shards(): lax.all_to_all(spectrum, 'stn', split_axis=2, concat_axis=1, tiled=True)]
  transfers between devices with their start and end apart: 3 -> 3, of which waited for: 3 -> 3; matrix products, arithmetic and copies ran while one was open for 1% -> 0% of each run, Pallas kernels for 0% -> 10%
where the time goes in v1:
time: 147 us; the launch traced here: 146 us
  waiting for transfers between devices  73.3 us (50%)
  Pallas kernels  44.2 us (30%)
  starting transfers between devices  17.5 us (12%)
  local copies, waits for them, and re-layouts  10.5 us (7%)
    all_to_all x2, waiting for transfers between devices, exchanged(): lax.all_to_all(flat, ('stn', 'tm'), split_axis=0, concat_axis=0, tiled=True)  44.3 us
    ppermute x1, waiting for transfers between devices, shards(): got = lax.ppermute(send, 'tm', [(0, 1), (1, 0)])  29 us
    pallas_call x2, Pallas kernels, spectra(): pl.pallas_call(functools.partial(spectra_kernel, tail), grid=(inputs // P...  27.7 us
    all_to_all x2, starting transfers between devices, exchanged(): lax.all_to_all(flat, ('stn', 'tm'), split_axis=0, concat_axis=0, tiled=True)  17.2 us
    pallas_call x1, Pallas kernels, gram(): pl.pallas_call(gram_kernel, grid_spec=pltpu.PrefetchScalarGridSpec(num_sc...  11.7 us
    unnamed x20, local copies, waits for them, and re-layouts  9.99 us
    pallas_call x1, Pallas kernels, fill(): pl.pallas_call(fill_kernel, grid_spec=pltpu.PrefetchScalarGridSpec(num_sc...  4.85 us
  transfers between devices with their start and end apart: 3, of which 3 were waited for; matrix products, arithmetic and copies ran while one was open for 0% of the time, Pallas kernels for 10%

profile of v1, /device:TPU:1, one launch (start us, length us, event | category | flops | bytes accessed | tf_op | source)
XLA Modules:
  0.0 145.7 jit_solution(391544663630586289)
XLA Ops:
  0.0 1.0 copy.15
  1.0 0.0 copy-start.4
  1.0 0.0 copy-start.5
  1.0 0.0 copy-start.6
  1.1 5.2 %copy.14 = bf16[4,8,512,128]{3,2,1,0:T(8,128)(2,1)} copy(bf16[4,8,512,128]{3,1,2,0:T(8,128)(2,1)} %bitcast.21) | data formatting | bytes 8388608
  6.3 13.5 %tail.1 = bf16[64,2,16,512]{3,2,1,0:T(8,128)(2,1)S(1)} custom-call(bf16[2,16,16,32,128]{4,3,2,1,0:T(8,128)(2,1)} %bitcast.22, f32[16,32,128]{2,1,0:T(8,128)S(1)} %bitcast.19, bf16[64,64]{1,0:T(8,128)(2,1)S(1)} %copy-done.6, f32[2,32,128]{2,1,0:T(8,128)S(1)} %copy-done.5, bf16[128,256]{1,0:T(8,128)(2,1)S(1)} %copy-done.4), custom_call_target="tpu_custom_call" | custom-call | flops 4000000000 | bytes 8388608 | tf_op jit(solution)/shard_map/tail/pallas_call | solution.py:100
  19.8 1.3 copy-done.2
  21.1 11.5 %all-to-all-start.1 = ((bf16[128,16,512]{2,1,0:T(8,128)(2,1)}), bf16[128,16,512]{2,1,0:T(8,128)(2,1)S(1)}, u32[]{:S(2)}, u32[]{:S(2)}) async-start(bf16[128,16,512]{2,1,0:T(8,128)(2,1)} %bitcast.18), calls=%async_computation.1 | async-start | bytes 4194304 | tf_op jit(solution)/shard_map/all_to_all | solution.py:225
  32.6 14.2 %head.1 = bf16[64,2,16,512]{3,2,1,0:T(8,128)(2,1)S(1)} custom-call(bf16[2,16,16,32,128]{4,3,2,1,0:T(8,128)(2,1)} %bitcast.23, f32[16,32,128]{2,1,0:T(8,128)S(1)} %bitcast.20, bf16[64,64]{1,0:T(8,128)(2,1)S(1)} %copy-done.6, f32[2,32,128]{2,1,0:T(8,128)S(1)} %copy-done.5, bf16[128,256]{1,0:T(8,128)(2,1)S(1)} %copy-done.4), custom_call_target="tpu_custom_call" | custom-call | flops 4000000000 | bytes 8388608 | tf_op jit(solution)/shard_map/head/pallas_call | solution.py:100
  46.8 0.0 copy-start.1
  46.8 1.3 copy-done.1
  48.1 14.8 %all-to-all-done.1 = bf16[128,16,512]{2,1,0:T(8,128)(2,1)S(1)} async-done(((bf16[128,16,512]{2,1,0:T(8,128)(2,1)}), bf16[128,16,512]{2,1,0:T(8,128)(2,1)S(1)}, u32[]{:S(2)}, u32[]{:S(2)}) %all-to-all-start.1) | async-done | bytes 2097184 | tf_op jit(solution)/shard_map/all_to_all | solution.py:225
  63.0 5.7 %all-to-all-start = ((bf16[128,16,512]{2,1,0:T(8,128)(2,1)}), bf16[128,16,512]{2,1,0:T(8,128)(2,1)}, u32[]{:S(2)}, u32[]{:S(2)}) async-start(bf16[128,16,512]{2,1,0:T(8,128)(2,1)} %bitcast.17), calls=%async_computation | async-start | bytes 4194304 | tf_op jit(solution)/shard_map/all_to_all | solution.py:225
  68.7 0.1 copy.11
  68.9 0.1 copy.12.row_ref
  68.9 0.1 broadcast_in_dim.16
  69.1 0.2 reshape_reshape.5.col_ref
  69.3 0.1 pad_add_fusion.info
  69.4 29.5 %all-to-all-done = bf16[128,16,512]{2,1,0:T(8,128)(2,1)} async-done(((bf16[128,16,512]{2,1,0:T(8,128)(2,1)}), bf16[128,16,512]{2,1,0:T(8,128)(2,1)}, u32[]{:S(2)}, u32[]{:S(2)}) %all-to-all-start) | async-done | bytes 2097184 | tf_op jit(solution)/shard_map/all_to_all | solution.py:225
  98.8 11.7 %gram.1 = (f32[2,10,2,128,256]{4,3,2,1,0:T(8,128)}, bf16[10,2,128,256]{3,2,1,0:T(8,128)(2,1)S(1)}) custom-call(s32[11]{0:T(128)S(1)} %pad_add_fusion.info, bf16[64,2,16,512]{3,2,1,0:T(8,128)(2,1)} %bitcast.3.main_ref, bf16[64,2,16,512]{3,2,1,0:T(8,128)(2,1)S(1)} %bitcast.16, s32[4,1,256]{2,1,0:T(1,128)S(1)} %copy.12.row_ref, ...), custom_call_target="tpu_custom_call" | custom-call | tf_op jit(solution)/shard_map/gram/pallas_call | solution.py:167
  110.5 0.3 collective-permute-start
  110.8 29.0 %collective-permute-done.got_ref = bf16[10,2,128,256]{3,2,1,0:T(8,128)(2,1)S(1)} collective-permute-done((bf16[10,2,128,256]{3,2,1,0:T(8,128)(2,1)S(1)}, bf16[10,2,128,256]{3,2,1,0:T(8,128)(2,1)S(1)}, u32[]{:S(2)}, u32[]{:S(2)}) %collective-permute-start) | collective-permute-done | bytes 1310752 | tf_op jit(solution)/shard_map/ppermute | solution.py:242
  139.7 1.1 copy-done.7
  140.8 4.8 %fill.1 = f32[2,10,2,128,256]{4,3,2,1,0:T(8,128)} custom-call(s32[11]{0:T(128)} %copy-done.3, f32[2,10,2,128,256]{4,3,2,1,0:T(8,128)} %get-tuple-element.7.whole_ref, bf16[10,2,128,256]{3,2,1,0:T(8,128)(2,1)} %copy-done.7), custom_call_target="tpu_custom_call", output_to_operand_aliasing={{}: (1, {})} | custom-call | tf_op jit(solution)/shard_map/fill/pallas_call | solution.py:205
  (14 shorter events, 0.1 us)
Async XLA Ops:
  0.0 68.7 %copy-start = (s32[2,512]{1,0:T(2,128)S(1)}, s32[2,512]{1,0:T(2,128)}, u32[]{:S(2)}) copy-start(s32[2,512]{1,0:T(2,128)} %param.9) | copy-start | bytes 12292
  1.0 5.3 %copy-start.4 = (bf16[128,256]{1,0:T(8,128)(2,1)S(1)}, bf16[128,256]{1,0:T(8,128)(2,1)}, u32[]{:S(2)}) copy-start(bf16[128,256]{1,0:T(8,128)(2,1)} %constant.22.clone.two_ref) | copy-start | bytes 196612
  1.0 5.3 %copy-start.5 = (f32[2,32,128]{2,1,0:T(8,128)S(1)}, f32[2,32,128]{2,1,0:T(8,128)}, u32[]{:S(2)}) copy-start(f32[2,32,128]{2,1,0:T(8,128)} %constant.21.clone.turn_ref) | copy-start | bytes 98308
  1.0 5.2 %copy-start.6 = (bf16[64,64]{1,0:T(8,128)(2,1)S(1)}, bf16[64,64]{1,0:T(8,128)(2,1)}, u32[]{:S(2)}) copy-start(bf16[64,64]{1,0:T(8,128)(2,1)} %constant.20.clone.one_ref) | copy-start | bytes 24580
  19.8 1.3 copy-start.2
  21.1 41.8 %all-to-all-start.1 = ((bf16[128,16,512]{2,1,0:T(8,128)(2,1)}), bf16[128,16,512]{2,1,0:T(8,128)(2,1)S(1)}, u32[]{:S(2)}, u32[]{:S(2)}) async-start(bf16[128,16,512]{2,1,0:T(8,128)(2,1)} %bitcast.18), calls=%async_computation.1 | async-start | bytes 4194304 | tf_op jit(solution)/shard_map/all_to_all | solution.py:225
  46.8 1.3 copy-start.1
  63.0 6.3 %copy-start.8 = (s32[2,10]{1,0:T(2,128)S(1)}, s32[2,10]{1,0:T(2,128)}, u32[]{:S(2)}) copy-start(s32[2,10]{1,0:T(2,128)} %param.10) | copy-start | bytes 244
  63.0 35.9 %all-to-all-start = ((bf16[128,16,512]{2,1,0:T(8,128)(2,1)}), bf16[128,16,512]{2,1,0:T(8,128)(2,1)}, u32[]{:S(2)}, u32[]{:S(2)}) async-start(bf16[128,16,512]{2,1,0:T(8,128)(2,1)} %bitcast.17), calls=%async_computation | async-start | bytes 4194304 | tf_op jit(solution)/shard_map/all_to_all | solution.py:225
  69.4 41.1 %copy-start.3 = (s32[11]{0:T(128)}, s32[11]{0:T(128)S(1)}, u32[]{:S(2)}) copy-start(s32[11]{0:T(128)S(1)} %pad_add_fusion.info) | copy-start | bytes 136
  110.5 29.3 %collective-permute-start = (bf16[10,2,128,256]{3,2,1,0:T(8,128)(2,1)S(1)}, bf16[10,2,128,256]{3,2,1,0:T(8,128)(2,1)S(1)}, u32[]{:S(2)}, u32[]{:S(2)}) collective-permute-start(bf16[10,2,128,256]{3,2,1,0:T(8,128)(2,1)S(1)} %get-tuple-element.8), channel_id=1, source_target_pairs={{0,1},{1,0},{2,3},{3,2},{4,5},{5,4},{6,7},{7,6},{8,9},{9,8},{10,11... | collective-permute-start | bytes 3932168 | tf_op jit(solution)/shard_map/ppermute | solution.py:242
  139.7 1.1 copy-start.7

commit v2 on v1

v2 whole, which is shorter than its diff:
```python
import jax
import jax.numpy as jnp
import numpy as np
from jax import lax
from jax.experimental import pallas as pl
from jax.experimental.pallas import tpu as pltpu
from jax.sharding import PartitionSpec as P


TAPS = 16
FFT = 4096
LANES = 128
ROWS = FFT // LANES
AVG = 16
F_DEV = 16
PART = 8


def tables():
    q = np.arange(ROWS)
    l = np.arange(LANES)
    angle = 2 * np.pi * np.outer(q, q) / ROWS
    one = np.block([[np.cos(angle), np.sin(angle)], [-np.sin(angle), np.cos(angle)]])
    angle = 2 * np.pi * np.outer(q, l) / FFT
    turn = np.stack([np.cos(angle), -np.sin(angle)])
    angle = 2 * np.pi * np.outer(np.arange(64) - 32, l) / LANES
    two = np.block([[np.cos(angle), np.sin(angle)], [-np.sin(angle), np.cos(angle)]]) / 64
    bf = jnp.bfloat16
    return jnp.asarray(one, bf), jnp.asarray(turn, jnp.float32), jnp.asarray(two, bf)


def head_taps(m):
    return [(t, m - TAPS + 1 + t) for t in range(TAPS) if m - TAPS + 1 + t >= 0]


def tail_taps(m):
    return [(t, m + 1 + t) for t in range(TAPS) if m + 1 + t < F_DEV]


PITCH = 72


def column(m, q):
    return pl.ds(pl.multiple_of(m * FFT + q * LANES, LANES), LANES)


def filtered(choose, x_ref, taps_ref, fir, q, planes):
    w = [jnp.broadcast_to(taps_ref[t : t + 1, column(0, q)], (PART, LANES)) for t in range(TAPS)]
    for n, c in enumerate(planes):
        x = [x_ref[n, :, column(m, q)].astype(jnp.float32) for m in range(F_DEV)]
        for m in range(F_DEV):
            total = jnp.zeros((PART, LANES), jnp.float32)
            for n, (t, frame) in enumerate(choose(m)):
                term = w[t] * x[frame]
                total = total + term if n else term
            fir[m, pl.ds(c * ROWS + q, PART, stride=PITCH), :] = total
        yield


def stage_one(fir, one_ref, turn_ref, mid, i, m):
    rows = pl.ds(pl.multiple_of(i * PITCH, 8), 2 * ROWS)
    frames = jnp.concatenate([fir[m, rows, :], fir[m + 1, rows, :]], axis=1)
    first = jnp.dot(one_ref[...], frames.astype(jnp.bfloat16), preferred_element_type=jnp.float32)
    for k in range(2):
        re = first[:ROWS, k * LANES : (k + 1) * LANES]
        im = first[ROWS:, k * LANES : (k + 1) * LANES]
        parts = (
            re * turn_ref[0] - im * turn_ref[1],
            re * turn_ref[1] + im * turn_ref[0],
        )
        for c in range(2):
            value = parts[c].astype(jnp.bfloat16)
            for h in range(2):
                row = h * 256 + (m + k) * AVG
                mid[row : row + AVG, c * LANES : (c + 1) * LANES] = value[h * AVG : (h + 1) * AVG]


def stage_two(two_ref, mid, spread, i, h):
    second = lax.dot_general(
        two_ref[...],
        mid[h * 256 : (h + 1) * 256, :],
        (((1,), (1,)), ((), ())),
        preferred_element_type=jnp.float32,
    )
    for c in range(2):
        for b in range(2):
            for j in range(0, 64, 8):
                spread[h, c, b, pl.ds(j * PART + i, 8, stride=PART), :] = second[
                    c * 64 + j : c * 64 + j + 8, b * LANES : (b + 1) * LANES
                ]


def put(spread, out_ref):
    for h in range(2):
        for c in range(2):
            for b in range(2):
                start = c * 256 + b * LANES
                out_ref[:, h, :, start : start + LANES] = (
                    spread[h, c, b].reshape(64, PART, LANES).astype(jnp.bfloat16)
                )


def filter_all(choose, x_ref, taps_ref, fir, planes):
    def body(q, carry):
        for _ in filtered(choose, x_ref, taps_ref, fir, q, planes):
            pass
        return carry

    lax.fori_loop(0, ROWS, body, 0)


def transform_all(tables, fir, spread, mids, out_ref, beside=None):
    one_ref, turn_ref, two_ref = tables
    width = 1 if beside else len(mids)

    def body(n, carry):
        other = beside(n) if beside else iter(())
        for m in range(0, F_DEV, 2):
            for k in range(width):
                stage_one(fir, one_ref, turn_ref, mids[k], n * width + k, m)
            next(other, None)
        for h in range(2):
            for k in range(width):
                stage_two(two_ref, mids[k], spread, n * width + k, h)
        for _ in other:
            pass
        return carry

    lax.fori_loop(0, PART // width, body, 0)
    put(spread, out_ref)


def first_kernel(x_ref, taps_ref, *refs):
    tables, (out_ref, fir, spread, *mids) = refs[:3], refs[3:]
    for c in range(2):
        pl.when(pl.program_id(0) == c)(
            lambda: filter_all(head_taps, x_ref, taps_ref, fir, (c,))
        )

    @pl.when(pl.program_id(0) == 1)
    def _():
        transform_all(tables, fir, spread, mids, out_ref)


def rest_kernel(x_ref, taps_ref, *refs):
    tables, (out_ref, fir, spread, *mids) = refs[:3], refs[3:6] + refs[7:]
    pair = (fir, refs[6])
    step = pl.program_id(0)

    @pl.when(step == 0)
    def _():
        filter_all(head_taps, x_ref, taps_ref, pair[0], (0, 1))

    for n in (1, 2):

        @pl.when(step == n)
        def _():
            def beside(i):
                for k in range(4):
                    q = i * 4 + k
                    yield from filtered(tail_taps, x_ref, taps_ref, pair[n % 2], q, (0, 1))

            transform_all(tables, pair[1 - n % 2], spread, mids, out_ref, beside)

    @pl.when(step == 3)
    def _():
        transform_all(tables, pair[0], spread, mids, out_ref)


def spectra(x, taps, consts, first):
    one, turn, two = consts
    steps, outs = (2, 1) if first else (4, 3)
    if first:
        pick = lambda g: (g, 0, 0)
    else:
        pick = lambda g: (0, jnp.where(g == 1, 0, 1), 0)
    whole = lambda a: pl.BlockSpec(a.shape, lambda g: (0,) * a.ndim)
    fir = pltpu.VMEM((F_DEV, PITCH * PART, LANES), jnp.float32)
    return pl.pallas_call(
        first_kernel if first else rest_kernel,
        grid=(steps,),
        in_specs=[
            pl.BlockSpec((1 if first else 2, PART, x.shape[2]), pick),
            whole(taps),
            whole(one),
            whole(turn),
            whole(two),
        ],
        out_specs=pl.BlockSpec((64, 2, PART, 512), lambda g: (0, 0, jnp.maximum(g - 1, 0), 0)),
        out_shape=jax.ShapeDtypeStruct((64, 2, PART * outs, 512), jnp.bfloat16),
        scratch_shapes=[fir, pltpu.VMEM((2, 2, 2, 64 * PART, LANES), jnp.float32)]
        + ([] if first else [fir])
        + [pltpu.VMEM((512, 256), jnp.bfloat16)] * 2,
        compiler_params=pltpu.CompilerParams(vmem_limit_bytes=60 << 20),
        cost_estimate=pl.CostEstimate(
            flops=outs * 2 * 10**9, bytes_accessed=outs * (4 << 20), transcendentals=0
        ),
        name="first" if first else "rest",
    )(x, taps, one, turn, two)


def gram_kernel(first_pair, early_ref, late_ref, late1_ref, row_ref, info, outs, left):
    out_ref, sends = outs[0], outs[1:]
    step = pl.program_id(0)

    @pl.when(step == 0)
    def _():
        for t in range(2):
            for h in range(2):
                rows = slice(h * PART, (h + 1) * PART)
                value = early_ref[:, t] if h == 0 else (late1_ref if t else late_ref)[:, 0, :PART]
                if t:
                    tail = late_ref[:, 0, PART * (1 + h) : PART * (2 + h)]
                    value = value.astype(jnp.float32) + tail.astype(jnp.float32)
                    value = value.astype(jnp.bfloat16)
                for c in range(2):
                    lane = (c * 2 + t) * 256
                    left[:, rows, lane : lane + 256] = value[:, :, c * 256 : (c + 1) * 256]

    pair = step + first_pair
    upper = sum((pair >= edge).astype(jnp.int32) for edge in (1, 3, 6))
    lower = pair - upper * (upper + 1) // 2
    mine = info[0]
    flag = info[1 + pair].astype(jnp.float32) * (1.0 / 512)

    def take(block, lanes):
        return left[block, :, lanes].reshape(-1, 512)

    halves = [pl.ds(upper * 16 + half * 8, 8) for half in (mine, 1 - mine)]
    rows = jnp.concatenate([take(b, lanes) for lanes in PLANES for b in halves], axis=0)
    right = pl.ds(lower * 16, 16)
    by_re, by_im = (
        lax.dot_general(
            rows,
            take(right, lanes),
            (((1,), (1,)), ((), ())),
            preferred_element_type=jnp.float32,
        )
        for lanes in PLANES
    )
    products = (by_re[:256] + by_im[256:], by_re[256:] - by_im[:256])
    ids = row_ref[lower]
    for other in range(2):
        start = pl.multiple_of((1 - mine if other else mine) * 128, 128)
        own = jnp.broadcast_to(row_ref[upper, :, pl.ds(start, 128)], (128, 128)).T
        weight = jnp.where(jnp.concatenate([own, own], axis=1) == ids, flag, 0.0)
        for c in range(2):
            value = products[c][other * 128 : (other + 1) * 128] * weight
            if not other:
                out_ref[0, 0, c] = value
                continue
            value = value.astype(jnp.bfloat16)
            begin = 0
            for send in sends:
                size = send[1]
                if len(sends) == 1:
                    send[0][0, c] = value
                else:

                    @pl.when((step >= begin) & (step < begin + size))
                    def _(ref=send[0]):
                        ref[0, c] = value

                begin += size


PLANES = (slice(0, 512), slice(512, 1024))


def gram(info, early, late, row_ids, first_pair, sizes, blocks, whole=None):
    many = blocks * 16
    aliased = whole is not None

    def kernel(info_ref, *refs):
        refs = refs[aliased:]
        outs = [refs[4]] + list(zip(refs[5 : 5 + len(sizes)], sizes))
        gram_kernel(first_pair, *refs[:4], info_ref, outs, refs[-1])

    def send_spec(begin, size):
        return pl.BlockSpec(
            (1, 2, 128, 256), lambda p, s: (jnp.clip(p - begin, 0, size - 1), 0, 0, 0)
        )

    one = pl.Buffered(1)
    begins = [sum(sizes[:n]) for n in range(len(sizes))]
    count = sum(sizes)
    return pl.pallas_call(
        kernel,
        grid_spec=pltpu.PrefetchScalarGridSpec(
            num_scalar_prefetch=1,
            grid=(count,),
            in_specs=[pl.BlockSpec(memory_space=pl.ANY)] * aliased
            + [
                pl.BlockSpec((many, 2, 8, 512), lambda p, s: (0, 0, 0, 0), pipeline_mode=one),
                pl.BlockSpec((many, 1, 24, 512), lambda p, s: (0, 0, 0, 0), pipeline_mode=one),
                pl.BlockSpec((many, 1, 8, 512), lambda p, s: (0, 1, 0, 0), pipeline_mode=one),
                pl.BlockSpec(row_ids.shape, lambda p, s: (0, 0, 0)),
            ],
            out_specs=[
                pl.BlockSpec(
                    (1, 1, 2, 128, 256), lambda p, s: (s[0], p + first_pair, 0, 0, 0)
                )
            ]
            + [send_spec(b, n) for b, n in zip(begins, sizes)],
            scratch_shapes=[pltpu.VMEM((many, 16, 1024), jnp.bfloat16)],
        ),
        out_shape=[jax.ShapeDtypeStruct((2, 10, 2, 128, 256), jnp.float32)]
        + [jax.ShapeDtypeStruct((n, 2, 128, 256), jnp.bfloat16) for n in sizes],
        input_output_aliases={1: 0} if aliased else {},
        compiler_params=pltpu.CompilerParams(vmem_limit_bytes=24 << 20),
        cost_estimate=pl.CostEstimate(
            flops=count * 27 * 10**7, bytes_accessed=blocks << 20, transcendentals=0
        ),
        name="gram",
    )(info, *([whole] if aliased else []), early, late, late, row_ids)


def fill_kernel(info, whole_ref, got_ref, out_ref):
    out_ref[0] = got_ref[...].astype(jnp.float32)


def fill(info, whole, got, first_pair):
    return pl.pallas_call(
        fill_kernel,
        grid_spec=pltpu.PrefetchScalarGridSpec(
            num_scalar_prefetch=1,
            grid=(got.shape[0],),
            in_specs=[
                pl.BlockSpec(memory_space=pl.ANY),
                pl.BlockSpec((1, 2, 128, 256), lambda p, s: (p, 0, 0, 0)),
            ],
            out_specs=pl.BlockSpec(
                (1, 1, 2, 128, 256), lambda p, s: (1 - s[0], p + first_pair, 0, 0, 0)
            ),
        ),
        out_shape=jax.ShapeDtypeStruct(whole.shape, whole.dtype),
        input_output_aliases={1: 0},
        compiler_params=pltpu.CompilerParams(vmem_limit_bytes=8 << 20),
        cost_estimate=pl.CostEstimate(
            flops=10**5, bytes_accessed=got.shape[0] * 786432, transcendentals=0
        ),
        name="fill",
    )(info, whole, got)


def exchanged(x):
    devices = lax.axis_size("stn") * lax.axis_size("tm")
    flat = x.reshape((devices,) + x.shape[2:])
    return lax.all_to_all(flat, ("stn", "tm"), split_axis=0, concat_axis=0, tiled=True).reshape(
        x.shape
    )


def swapped(x):
    return lax.ppermute(x, "tm", [(0, 1), (1, 0)])


def shards(voltages, filter_taps, membership, block_active):
    mine = lax.axis_index("tm")
    consts = tables()
    early = exchanged(spectra(voltages, filter_taps, consts, True))
    late = exchanged(spectra(voltages, filter_taps, consts, False))
    ids = jnp.repeat(lax.dynamic_index_in_dim(membership, mine, 0, keepdims=False), 2)
    flags = lax.dynamic_index_in_dim(block_active, mine, 0, keepdims=False)
    info = jnp.concatenate([mine.astype(jnp.int32)[None], flags])
    ids = ids.reshape(4, 1, 256)
    whole, send = gram(info, early, late, ids, 0, (3,), 2)
    gots = [swapped(send)]
    whole, *sends = gram(info, early, late, ids, 3, (5, 2), 4, whole)
    gots += [swapped(send) for send in sends]
    for first_pair, got in zip((0, 3, 8), gots):
        whole = fill(info, whole, got, first_pair)
    return whole


def solution(mesh):
    placed = (P(None, "stn", "tm"), P(), P("stn", None), P("stn", None))
    return jax.shard_map(
        shards,
        mesh=mesh,
        in_specs=placed,
        out_specs=P("stn", None, None, "tm", None),
        check_vma=False,
    )
```

time: 147 us -> 134 us (0.912)
  waiting for transfers between devices: 73.3 us -> 63.7 us
  local copies, waits for them, and re-layouts: 10.5 us -> 2.45 us
  starting transfers between devices: 17.5 us -> 23 us
    unnamed x20 -> x8, local copies, waits for them, and re-layouts: 9.99 us -> 2.2 us
    ppermute x1 -> x3, waiting for transfers between devices: 29 us -> 22.6 us  [swapped(): return lax.ppermute(x, 'tm', [(0, 1), (1, 0)])]
    all_to_all x2, starting transfers between devices: 17.2 us -> 21.2 us  [exchanged(): lax.all_to_all(flat, ('stn', 'tm'), split_axis=0, concat_axis=0, tiled=True)]
    all_to_all x2, waiting for transfers between devices: 44.3 us -> 41.1 us  [exchanged(): lax.all_to_all(flat, ('stn', 'tm'), split_axis=0, concat_axis=0, tiled=True)]
    pallas_call x3 -> x4, Pallas kernels: 39.3 us -> 37 us  [the longest x2 27.9 us: spectra(): pl.pallas_call(first_kernel if first else rest_kernel, grid=(steps,), in_...]
    pallas_call x1 -> x3, Pallas kernels: 4.85 us -> 6.1 us  [fill(): pl.pallas_call(fill_kernel, grid_spec=pltpu.PrefetchScalarGridSpec(num_sc...]
  transfers between devices with their start and end apart: 3 -> 5, of which waited for: 3 -> 3; matrix products, arithmetic and copies ran while one was open for 0% -> 0% of each run, Pallas kernels for 10% -> 19%
where the time goes in v2:
time: 134 us; the launch traced here: 132 us
  waiting for transfers between devices  63.7 us (48%)
  Pallas kernels  43.1 us (32%)
  starting transfers between devices  23 us (17%)
  local copies, waits for them, and re-layouts  2.45 us (2%)
    all_to_all x2, waiting for transfers between devices, exchanged(): lax.all_to_all(flat, ('stn', 'tm'), split_axis=0, concat_axis=0, tiled=True)  41.1 us
    pallas_call x2, Pallas kernels, spectra(): pl.pallas_call(first_kernel if first else rest_kernel, grid=(steps,), in_...  27.9 us
    ppermute x3, waiting for transfers between devices, swapped(): return lax.ppermute(x, 'tm', [(0, 1), (1, 0)])  22.6 us
    all_to_all x2, starting transfers between devices, exchanged(): lax.all_to_all(flat, ('stn', 'tm'), split_axis=0, concat_axis=0, tiled=True)  21.2 us
    pallas_call x2, Pallas kernels, gram(): pl.pallas_call(kernel, grid_spec=pltpu.PrefetchScalarGridSpec(num_scalar_...  9.08 us
    pallas_call x3, Pallas kernels, fill(): pl.pallas_call(fill_kernel, grid_spec=pltpu.PrefetchScalarGridSpec(num_sc...  6.1 us
  transfers between devices with their start and end apart: 5, of which 3 were waited for; matrix products, arithmetic and copies ran while one was open for 0% of the time, Pallas kernels for 19%

profile of v2, /device:TPU:1, one launch (start us, length us, event | category | flops | bytes accessed | tf_op | source)
XLA Modules:
  0.0 132.4 jit_solution(5237387693247862629)
XLA Ops:
  0.0 0.0 copy-start
  0.0 7.9 %first.1 = bf16[64,2,8,512]{3,2,1,0:T(8,128)(2,1)} custom-call(bf16[2,16,65536]{2,1,0:T(8,128)(2,1)} %x_ref.3, f32[16,4096]{1,0:T(8,128)} %taps_ref.3, bf16[64,64]{1,0:T(8,128)(2,1)} %constant.20.clone.refs_0_, f32[2,32,128]{2,1,0:T(8,128)} %constant.21.clone.refs_1_, bf16[128,256]{1,0:T(8,128)(2,1)} %constant.22.clone.refs_2_), custom_call_target="tpu_custom_call" | custom-call | flops 2000000000 | bytes 4194304 | tf_op jit(solution)/shard_map/first/pallas_call | solution.py:179
  7.9 11.5 %all-to-all-start = ((bf16[128,8,512]{2,1,0:T(8,128)(2,1)}), bf16[128,8,512]{2,1,0:T(8,128)(2,1)S(1)}, u32[]{:S(2)}, u32[]{:S(2)}) async-start(bf16[128,8,512]{2,1,0:T(8,128)(2,1)} %bitcast.16), calls=%async_computation | async-start | bytes 2097152 | tf_op jit(solution)/shard_map/all_to_all | solution.py:349
  19.4 20.0 %rest.1 = bf16[64,2,24,512]{3,2,1,0:T(8,128)(2,1)} custom-call(bf16[2,16,65536]{2,1,0:T(8,128)(2,1)} %x_ref.3, f32[16,4096]{1,0:T(8,128)} %taps_ref.3, bf16[64,64]{1,0:T(8,128)(2,1)} %constant.20.clone.refs_0_, f32[2,32,128]{2,1,0:T(8,128)} %constant.21.clone.refs_1_, bf16[128,256]{1,0:T(8,128)(2,1)} %constant.22.clone.refs_2_), custom_call_target="tpu_custom_call" | custom-call | flops 6000000000 | bytes 12582912 | tf_op jit(solution)/shard_map/rest/pallas_call | solution.py:179
  39.4 0.0 all-to-all-done
  39.4 1.0 copy-done.1
  40.4 9.8 %all-to-all-start.1 = ((bf16[128,24,512]{2,1,0:T(8,128)(2,1)}), bf16[128,24,512]{2,1,0:T(8,128)(2,1)S(1)}, u32[]{:S(2)}, u32[]{:S(2)}) async-start(bf16[128,24,512]{2,1,0:T(8,128)(2,1)} %bitcast.15), calls=%async_computation.1 | async-start | bytes 6291456 | tf_op jit(solution)/shard_map/all_to_all | solution.py:349
  50.2 0.0 copy-done
  50.2 0.1 copy.14
  50.4 0.1 copy.15.refs_3_.refs_4_
  50.5 0.1 pad_add_fusion.info_ref.info
  50.5 41.1 %all-to-all-done.1 = bf16[128,24,512]{2,1,0:T(8,128)(2,1)S(1)} async-done(((bf16[128,24,512]{2,1,0:T(8,128)(2,1)}), bf16[128,24,512]{2,1,0:T(8,128)(2,1)S(1)}, u32[]{:S(2)}, u32[]{:S(2)}) %all-to-all-start.1) | async-done | bytes 3145760 | tf_op jit(solution)/shard_map/all_to_all | solution.py:349
  91.6 1.2 copy-done.2
  92.8 3.1 %gram.2 = (f32[2,10,2,128,256]{4,3,2,1,0:T(8,128)}, bf16[3,2,128,256]{3,2,1,0:T(8,128)(2,1)S(1)}) custom-call(s32[11]{0:T(128)S(1)} %pad_add_fusion.info_ref.info, bf16[64,2,8,512]{3,2,1,0:T(8,128)(2,1)S(1)} %bitcast.13, bf16[64,2,24,512]{3,2,1,0:T(8,128)(2,1)S(1)} %bitcast.9, bf16[64,2,24,512]{3,2,1,0:T(8,128)(2,1)S(1)} %bitcast.10, ...), custom_call_target="tpu_custom_call" | custom-call | flops 810000000 | bytes 2097152 | tf_op jit(solution)/shard_map/gram/pallas_call | solution.py:287
  95.9 6.0 %gram.3 = (f32[2,10,2,128,256]{4,3,2,1,0:T(8,128)}, bf16[5,2,128,256]{3,2,1,0:T(8,128)(2,1)S(1)}, bf16[2,2,128,256]{3,2,1,0:T(8,128)(2,1)S(1)}) custom-call(s32[11]{0:T(128)S(1)} %pad_add_fusion.info_ref.info, f32[2,10,2,128,256]{4,3,2,1,0:T(8,128)} %get-tuple-element.10.refs_0_, ...), custom_call_target="tpu_custom_call", output_to_operand_aliasing={{0}: (1, {})} | custom-call | flops 1890000000 | bytes 4194304 | tf_op jit(solution)/shard_map/gram/pallas_call | solution.py:287
  101.9 0.3 collective-permute-start.1
  102.2 1.2 collective-permute-start
  103.4 0.3 collective-permute-start.2
  103.7 21.7 %collective-permute-done.got_ref = bf16[3,2,128,256]{3,2,1,0:T(8,128)(2,1)S(1)} collective-permute-done((bf16[3,2,128,256]{3,2,1,0:T(8,128)(2,1)S(1)}, bf16[3,2,128,256]{3,2,1,0:T(8,128)(2,1)S(1)}, u32[]{:S(2)}, u32[]{:S(2)}) %collective-permute-start) | collective-permute-done | bytes 393248 | tf_op jit(solution)/shard_map/ppermute | solution.py:355
  125.4 2.0 %fill.3.whole_ref = f32[2,10,2,128,256]{4,3,2,1,0:T(8,128)} custom-call(s32[11]{0:T(128)S(1)} %pad_add_fusion.info_ref.info, f32[2,10,2,128,256]{4,3,2,1,0:T(8,128)} %get-tuple-element.11.whole_ref, bf16[3,2,128,256]{3,2,1,0:T(8,128)(2,1)S(1)} %collective-permute-done.got_ref), custom_call_target="tpu_custom_call", output_to_operand_aliasing={{}: (1, {})} | custom-call | flops 100000 | bytes 2359296 | tf_op jit(solution)/shard_map/fill/pallas_call | solution.py:323
  127.4 0.0 collective-permute-done.1.got_ref
  127.4 2.7 %fill.4.whole_ref = f32[2,10,2,128,256]{4,3,2,1,0:T(8,128)} custom-call(s32[11]{0:T(128)S(1)} %pad_add_fusion.info_ref.info, f32[2,10,2,128,256]{4,3,2,1,0:T(8,128)} %fill.3.whole_ref, bf16[5,2,128,256]{3,2,1,0:T(8,128)(2,1)S(1)} %collective-permute-done.1.got_ref), custom_call_target="tpu_custom_call", output_to_operand_aliasing={{}: (1, {})} | custom-call | flops 100000 | bytes 3932160 | tf_op jit(solution)/shard_map/fill/pallas_call | solution.py:323
  130.1 0.9 collective-permute-done.2.got_ref
  131.0 1.4 %fill.5 = f32[2,10,2,128,256]{4,3,2,1,0:T(8,128)} custom-call(s32[11]{0:T(128)S(1)} %pad_add_fusion.info_ref.info, f32[2,10,2,128,256]{4,3,2,1,0:T(8,128)} %fill.4.whole_ref, bf16[2,2,128,256]{3,2,1,0:T(8,128)(2,1)S(1)} %collective-permute-done.2.got_ref), custom_call_target="tpu_custom_call", output_to_operand_aliasing={{}: (1, {})} | custom-call | flops 100000 | bytes 1572864 | tf_op jit(solution)/shard_map/fill/pallas_call | solution.py:323
  (7 shorter events, 0.1 us)
Async XLA Ops:
  0.0 50.2 %copy-start = (s32[2,512]{1,0:T(2,128)S(1)}, s32[2,512]{1,0:T(2,128)}, u32[]{:S(2)}) copy-start(s32[2,512]{1,0:T(2,128)} %param.9) | copy-start | bytes 12292
  7.9 31.5 %all-to-all-start = ((bf16[128,8,512]{2,1,0:T(8,128)(2,1)}), bf16[128,8,512]{2,1,0:T(8,128)(2,1)S(1)}, u32[]{:S(2)}, u32[]{:S(2)}) async-start(bf16[128,8,512]{2,1,0:T(8,128)(2,1)} %bitcast.16), calls=%async_computation | async-start | bytes 2097152 | tf_op jit(solution)/shard_map/all_to_all | solution.py:349
  39.4 11.0 %copy-start.3 = (s32[2,10]{1,0:T(2,128)S(1)}, s32[2,10]{1,0:T(2,128)}, u32[]{:S(2)}) copy-start(s32[2,10]{1,0:T(2,128)} %param.10) | copy-start | bytes 244
  39.4 1.0 copy-start.1
  40.4 51.2 %all-to-all-start.1 = ((bf16[128,24,512]{2,1,0:T(8,128)(2,1)}), bf16[128,24,512]{2,1,0:T(8,128)(2,1)S(1)}, u32[]{:S(2)}, u32[]{:S(2)}) async-start(bf16[128,24,512]{2,1,0:T(8,128)(2,1)} %bitcast.15), calls=%async_computation.1 | async-start | bytes 6291456 | tf_op jit(solution)/shard_map/all_to_all | solution.py:349
  91.6 1.2 copy-start.2
  101.9 25.5 %collective-permute-start.1 = (bf16[5,2,128,256]{3,2,1,0:T(8,128)(2,1)S(1)}, bf16[5,2,128,256]{3,2,1,0:T(8,128)(2,1)S(1)}, u32[]{:S(2)}, u32[]{:S(2)}) collective-permute-start(bf16[5,2,128,256]{3,2,1,0:T(8,128)(2,1)S(1)} %get-tuple-element.13), channel_id=1, source_target_pairs={{0,1},{1,0},{2,3},{3,2},{4,5},{5,4},{6,7},{7,6},{8,9},{9,8},{10,11... | collective-permute-start | bytes 1966088 | tf_op jit(solution)/shard_map/ppermute | solution.py:355
  102.2 23.2 %collective-permute-start = (bf16[3,2,128,256]{3,2,1,0:T(8,128)(2,1)S(1)}, bf16[3,2,128,256]{3,2,1,0:T(8,128)(2,1)S(1)}, u32[]{:S(2)}, u32[]{:S(2)}) collective-permute-start(bf16[3,2,128,256]{3,2,1,0:T(8,128)(2,1)S(1)} %get-tuple-element.12), channel_id=1, source_target_pairs={{0,1},{1,0},{2,3},{3,2},{4,5},{5,4},{6,7},{7,6},{8,9},{9,8},{10,11... | collective-permute-start | bytes 1179656 | tf_op jit(solution)/shard_map/ppermute | solution.py:355
  103.4 27.6 %collective-permute-start.2 = (bf16[2,2,128,256]{3,2,1,0:T(8,128)(2,1)S(1)}, bf16[2,2,128,256]{3,2,1,0:T(8,128)(2,1)S(1)}, u32[]{:S(2)}, u32[]{:S(2)}) collective-permute-start(bf16[2,2,128,256]{3,2,1,0:T(8,128)(2,1)S(1)} %get-tuple-element.14), channel_id=1, source_target_pairs={{0,1},{1,0},{2,3},{3,2},{4,5},{5,4},{6,7},{7,6},{8,9},{9,8},{10,11... | collective-permute-start | bytes 786440 | tf_op jit(solution)/shard_map/ppermute | solution.py:355

commit v3 on v2

v3 whole, which is shorter than its diff:
```python
import functools
import itertools

import jax
import jax.numpy as jnp
import numpy as np
from jax import lax
from jax.experimental import pallas as pl
from jax.experimental.pallas import tpu as pltpu
from jax.sharding import PartitionSpec as P


TAPS = 16
FFT = 4096
LANES = 128
ROWS = FFT // LANES
AVG = 16
F_DEV = 16
PART = 8


def tables():
    q = np.arange(ROWS)
    l = np.arange(LANES)
    angle = 2 * np.pi * np.outer(q, q) / ROWS
    one = np.block([[np.cos(angle), np.sin(angle)], [-np.sin(angle), np.cos(angle)]])
    angle = 2 * np.pi * np.outer(q, l) / FFT
    turn = np.stack([np.cos(angle), -np.sin(angle)])
    angle = 2 * np.pi * np.outer(np.arange(64) - 32, l) / LANES
    two = np.block([[np.cos(angle), np.sin(angle)], [-np.sin(angle), np.cos(angle)]]) / 64
    bf = jnp.bfloat16
    return jnp.asarray(one, bf), jnp.asarray(turn, jnp.float32), jnp.asarray(two, bf)


HALF = F_DEV // 2


def head_taps(m):
    return [(t, m - TAPS + 1 + t) for t in range(TAPS) if m - TAPS + 1 + t >= 0]


def tail_taps(m):
    return [(t, m + 1 + t) for t in range(TAPS) if m + 1 + t < F_DEV]


LOW_HEAD = (head_taps, 0, range(0, HALF))
HIGH_HEAD = (head_taps, HALF, range(0, F_DEV))
LOW_TAIL = (tail_taps, 0, range(0, F_DEV))
HIGH_TAIL = (tail_taps, HALF, range(HALF, F_DEV))

VMEM_ALL = 67043328
FIRST = ((LOW_HEAD, 0), (LOW_HEAD, 1), (HIGH_TAIL, 0))
REST = ((HIGH_HEAD, 0), (LOW_TAIL, 0), (LOW_TAIL, 1), (HIGH_HEAD, 1), (HIGH_TAIL, 1))


PITCH = 72


def column(m, q):
    return pl.ds(pl.multiple_of(m * FFT + q * LANES, LANES), LANES)


def filtered(kind, origin, x_ref, taps_ref, fir, q):
    choose, start, used = kind
    w = [jnp.broadcast_to(taps_ref[t : t + 1, column(0, q)], (PART, LANES)) for t in range(TAPS)]
    for c in range(2):
        x = {m: x_ref[c, :, column(m - origin, q)].astype(jnp.float32) for m in used}
        for m in range(HALF):
            total = jnp.zeros((PART, LANES), jnp.float32)
            for n, (t, frame) in enumerate(choose(start + m)):
                term = w[t] * x[frame]
                total = total + term if n else term
            fir[m, pl.ds(c * ROWS + q, PART, stride=PITCH), :] = total


def stage_one(fir, one_ref, turn_ref, mid, i, m):
    rows = pl.ds(pl.multiple_of(i * PITCH, 8), 2 * ROWS)
    frames = jnp.concatenate([fir[m, rows, :], fir[m + 1, rows, :]], axis=1)
    first = jnp.dot(one_ref[...], frames.astype(jnp.bfloat16), preferred_element_type=jnp.float32)
    for k in range(2):
        re = first[:ROWS, k * LANES : (k + 1) * LANES]
        im = first[ROWS:, k * LANES : (k + 1) * LANES]
        parts = (
            re * turn_ref[0] - im * turn_ref[1],
            re * turn_ref[1] + im * turn_ref[0],
        )
        for c in range(2):
            value = parts[c].astype(jnp.bfloat16)
            for h in range(2):
                row = h * LANES + (m + k) * AVG
                mid[row : row + AVG, c * LANES : (c + 1) * LANES] = value[h * AVG : (h + 1) * AVG]


def stage_two(two_ref, mid, spread, i):
    second = lax.dot_general(
        two_ref[...],
        mid[...],
        (((1,), (1,)), ((), ())),
        preferred_element_type=jnp.float32,
    )
    for h in range(2):
        for c in range(2):
            for j in range(0, 64, 8):
                spread[h, c, pl.ds(j * PART + i, 8, stride=PART), :] = second[
                    c * 64 + j : c * 64 + j + 8, h * LANES : (h + 1) * LANES
                ]


def filter_all(kind, origin, x_ref, taps_ref, fir):
    together = 4 if len(kind[2]) == HALF else 2

    def body(n, carry):
        for k in range(together):
            filtered(kind, origin, x_ref, taps_ref, fir, n * together + k)
        return carry

    lax.fori_loop(0, ROWS // together, body, 0)


def transform_all(tables, fir, spread, mids, out_ref):
    one_ref, turn_ref, two_ref = tables
    depth = 2
    for i in range(PART + depth):
        if i < PART:
            for m in range(0, HALF, 2):
                stage_one(fir, one_ref, turn_ref, mids[i], i, m)
        if i >= depth:
            stage_two(two_ref, mids[i - depth], spread, i - depth)
    for h in range(2):
        for c in range(2):
            out_ref[:, h, :, c * LANES : (c + 1) * LANES] = (
                spread[h, c].reshape(64, PART, LANES).astype(jnp.bfloat16)
            )


def spectra_kernel(units, width, x_ref, taps_ref, *refs):
    tables, (out_ref, fir, spread, *mids) = refs[:3], refs[3:]
    step = pl.program_id(0)
    for kind in {unit[0]: None for unit in units}:
        here = functools.reduce(
            jnp.logical_or, [step == n for n, unit in enumerate(units) if unit[0] == kind]
        )
        origin = kind[2][0] if width < F_DEV else 0

        @pl.when(here)
        def _():
            filter_all(kind, origin, x_ref, taps_ref, fir)

    transform_all(tables, fir, spread, mids, out_ref)


def listed(values, g):
    return sum(value * (g == n).astype(jnp.int32) for n, value in enumerate(values))


def spectra(x, taps, consts, units):
    one, turn, two = consts
    width = max(len(kind[2]) for kind, _ in units)
    whole = lambda a: pl.BlockSpec(a.shape, lambda g: (0,) * a.ndim)

    def pick(g):
        side = [kind[2][0] // HALF if width < F_DEV else 0 for kind, _ in units]
        return (0, listed([group for _, group in units], g), listed(side, g))

    block = (64, 2, PART, 2 * LANES)
    return pl.pallas_call(
        functools.partial(spectra_kernel, units, width),
        grid=(len(units),),
        in_specs=[
            pl.BlockSpec((2, PART, width * FFT), pick),
            whole(taps),
            whole(one),
            whole(turn),
            whole(two),
        ],
        out_specs=pl.BlockSpec(block, lambda g: (0, 0, 0, g)),
        out_shape=jax.ShapeDtypeStruct(block[:3] + (block[3] * len(units),), jnp.bfloat16),
        scratch_shapes=[
            pltpu.VMEM((HALF, PITCH * PART, LANES), jnp.float32),
            pltpu.VMEM((2, 2, 64 * PART, LANES), jnp.float32),
        ]
        + [pltpu.VMEM((2 * LANES, 2 * LANES), jnp.bfloat16)] * PART,
        compiler_params=pltpu.CompilerParams(vmem_limit_bytes=VMEM_ALL),
        cost_estimate=pl.CostEstimate(
            flops=len(units) * 10**9, bytes_accessed=len(units) << 21, transcendentals=0
        ),
    )(x, taps, one, turn, two)


def gram_kernel(first_pair, early_ref, late_ref, row_ref, info, outs, left):
    out_ref, sends = outs[0], outs[1:]
    step = pl.program_id(0)

    def arrived(kind, group, t, c):
        ref, units = (early_ref, FIRST) if (kind, group) in FIRST else (late_ref, REST)
        lane = (units.index((kind, group)) * 2 + c) * LANES
        return ref[:, t, :, lane : lane + LANES]

    @pl.when(step == 0)
    def _():
        kinds = ((LOW_HEAD, LOW_TAIL), (HIGH_HEAD, HIGH_TAIL))
        for c, t, h, group in itertools.product(range(2), repeat=4):
            head, tail = kinds[h]
            value = arrived(head, group, t, c)
            if t:
                more = arrived(tail, group, 0, c).astype(jnp.float32)
                value = (value.astype(jnp.float32) + more).astype(jnp.bfloat16)
            lane = (c * 4 + t * 2 + h) * LANES
            left[:, group * PART : (group + 1) * PART, lane : lane + LANES] = value

    pair = step + first_pair
    upper = sum((pair >= edge).astype(jnp.int32) for edge in (1, 3, 6))
    lower = pair - upper * (upper + 1) // 2
    mine = info[0]
    flag = info[1 + pair].astype(jnp.float32) * (1.0 / 512)

    def take(block, lanes):
        return left[block, :, lanes].reshape(-1, 512)

    halves = [pl.ds(upper * 16 + half * 8, 8) for half in (mine, 1 - mine)]
    rows = jnp.concatenate([take(b, lanes) for lanes in PLANES for b in halves], axis=0)
    right = pl.ds(lower * 16, 16)
    by_re, by_im = (
        lax.dot_general(
            rows,
            take(right, lanes),
            (((1,), (1,)), ((), ())),
            preferred_element_type=jnp.float32,
        )
        for lanes in PLANES
    )
    products = (by_re[:256] + by_im[256:], by_re[256:] - by_im[:256])
    ids = row_ref[lower]
    for other in range(2):
        start = pl.multiple_of((1 - mine if other else mine) * 128, 128)
        own = jnp.broadcast_to(row_ref[upper, :, pl.ds(start, 128)], (128, 128)).T
        weight = jnp.where(jnp.concatenate([own, own], axis=1) == ids, flag, 0.0)
        for c in range(2):
            value = products[c][other * 128 : (other + 1) * 128] * weight
            if not other:
                out_ref[0, 0, c] = value
                continue
            value = value.astype(jnp.bfloat16)
            begin = 0
            for send in sends:
                size = send[1]
                if len(sends) == 1:
                    send[0][0, c] = value
                else:

                    @pl.when((step >= begin) & (step < begin + size))
                    def _(ref=send[0]):
                        ref[0, c] = value

                begin += size


PLANES = (slice(0, 512), slice(512, 1024))


def gram(info, early, late, row_ids, first_pair, sizes, blocks, whole=None):
    many = blocks * 16
    aliased = whole is not None

    def kernel(info_ref, *refs):
        refs = refs[aliased:]
        outs = [refs[3]] + list(zip(refs[4 : 4 + len(sizes)], sizes))
        gram_kernel(first_pair, *refs[:3], info_ref, outs, refs[-1])

    def send_spec(begin, size):
        return pl.BlockSpec(
            (1, 2, 128, 256), lambda p, s: (jnp.clip(p - begin, 0, size - 1), 0, 0, 0)
        )

    one = pl.Buffered(1)
    begins = [sum(sizes[:n]) for n in range(len(sizes))]
    count = sum(sizes)
    return pl.pallas_call(
        kernel,
        grid_spec=pltpu.PrefetchScalarGridSpec(
            num_scalar_prefetch=1,
            grid=(count,),
            in_specs=[pl.BlockSpec(memory_space=pl.ANY)] * aliased
            + [
                pl.BlockSpec(
                    (many,) + x.shape[1:], lambda p, s: (0, 0, 0, 0), pipeline_mode=one
                )
                for x in (early, late)
            ]
            + [
                pl.BlockSpec(row_ids.shape, lambda p, s: (0, 0, 0)),
            ],
            out_specs=[
                pl.BlockSpec(
                    (1, 1, 2, 128, 256), lambda p, s: (s[0], p + first_pair, 0, 0, 0)
                )
            ]
            + [send_spec(b, n) for b, n in zip(begins, sizes)],
            scratch_shapes=[pltpu.VMEM((many, 16, 1024), jnp.bfloat16)],
        ),
        out_shape=[jax.ShapeDtypeStruct((2, 10, 2, 128, 256), jnp.float32)]
        + [jax.ShapeDtypeStruct((n, 2, 128, 256), jnp.bfloat16) for n in sizes],
        input_output_aliases={1: 0} if aliased else {},
        compiler_params=pltpu.CompilerParams(vmem_limit_bytes=24 << 20),
        cost_estimate=pl.CostEstimate(
            flops=count * 27 * 10**7, bytes_accessed=blocks << 20, transcendentals=0
        ),
        name="gram",
    )(info, *([whole] if aliased else []), early, late, row_ids)


def fill_kernel(info, whole_ref, got_ref, out_ref):
    out_ref[0] = got_ref[...].astype(jnp.float32)


def fill(info, whole, got, first_pair):
    return pl.pallas_call(
        fill_kernel,
        grid_spec=pltpu.PrefetchScalarGridSpec(
            num_scalar_prefetch=1,
            grid=(got.shape[0],),
            in_specs=[
                pl.BlockSpec(memory_space=pl.ANY),
                pl.BlockSpec((1, 2, 128, 256), lambda p, s: (p, 0, 0, 0)),
            ],
            out_specs=pl.BlockSpec(
                (1, 1, 2, 128, 256), lambda p, s: (1 - s[0], p + first_pair, 0, 0, 0)
            ),
        ),
        out_shape=jax.ShapeDtypeStruct(whole.shape, whole.dtype),
        input_output_aliases={1: 0},
        compiler_params=pltpu.CompilerParams(vmem_limit_bytes=8 << 20),
        cost_estimate=pl.CostEstimate(
            flops=10**5, bytes_accessed=got.shape[0] * 786432, transcendentals=0
        ),
        name="fill",
    )(info, whole, got)


def exchanged(x):
    devices = lax.axis_size("stn") * lax.axis_size("tm")
    flat = x.reshape((devices,) + x.shape[2:])
    flat = lax.all_to_all(flat, ("stn", "tm"), split_axis=0, concat_axis=0, tiled=True)
    return flat.reshape(x.shape)


def swapped(x):
    return lax.ppermute(x, "tm", [(0, 1), (1, 0)])


def shards(voltages, filter_taps, membership, block_active):
    mine = lax.axis_index("tm")
    consts = tables()
    ids = jnp.repeat(lax.dynamic_index_in_dim(membership, mine, 0, keepdims=False), 2)
    flags = lax.dynamic_index_in_dim(block_active, mine, 0, keepdims=False)
    info = jnp.concatenate([mine.astype(jnp.int32)[None], flags])
    ids = ids.reshape(4, 1, 256)
    early = exchanged(spectra(voltages, filter_taps, consts, FIRST))
    late = spectra(voltages, filter_taps, consts, REST)
    late = exchanged(late)
    whole, send = gram(info, early, late, ids, 0, (3,), 2)
    gots = [swapped(send)]
    whole, *sends = gram(info, early, late, ids, 3, (5, 2), 4, whole)
    gots += [swapped(send) for send in sends]
    for first_pair, got in zip((0, 3, 8), gots):
        whole = fill(info, whole, got, first_pair)
    return whole


def solution(mesh):
    placed = (P(None, "stn", "tm"), P(), P("stn", None), P("stn", None))
    return jax.shard_map(
        shards,
        mesh=mesh,
        in_specs=placed,
        out_specs=P("stn", None, None, "tm", None),
        check_vma=False,
    )
```

time: 134 us -> 128 us (0.955)
  starting transfers between devices: 23 us -> 18.1 us
  waiting for transfers between devices: 63.7 us -> 67.3 us
  Pallas kernels: 43.1 us -> 40.5 us
  local copies, waits for them, and re-layouts: 2.45 us -> 0.26 us
    pallas_call x2, Pallas kernels: 27.9 us -> 22.7 us  [spectra(): pl.pallas_call(functools.partial(spectra_kernel, units, width), grid=(len...]
    all_to_all x2, starting transfers between devices: 21.2 us -> 16.3 us  [exchanged(): lax.all_to_all(flat, ('stn', 'tm'), split_axis=0, concat_axis=0, tiled=True)]
    all_to_all x2, waiting for transfers between devices: 41.1 us -> 44.6 us  [exchanged(): lax.all_to_all(flat, ('stn', 'tm'), split_axis=0, concat_axis=0, tiled=True)]
    pallas_call x2, Pallas kernels: 9.08 us -> 11.7 us  [gram(): pl.pallas_call(kernel, grid_spec=pltpu.PrefetchScalarGridSpec(num_scalar_...]
    unnamed x8 -> x4, local copies, waits for them, and re-layouts: 2.2 us -> 0.01 us
  transfers between devices with their start and end apart: 5 -> 5, of which waited for: 3 -> 4; matrix products, arithmetic and copies ran while one was open for 0% -> 0% of each run, Pallas kernels for 19% -> 16%
where the time goes in v3:
time: 128 us; the launch traced here: 126 us
  waiting for transfers between devices  67.3 us (53%)
  Pallas kernels  40.5 us (32%)
  starting transfers between devices  18.1 us (14%)
    all_to_all x2, waiting for transfers between devices, exchanged(): lax.all_to_all(flat, ('stn', 'tm'), split_axis=0, concat_axis=0, tiled=True)  44.6 us
    pallas_call x2, Pallas kernels, spectra(): pl.pallas_call(functools.partial(spectra_kernel, units, width), grid=(len...  22.7 us
    ppermute x3, waiting for transfers between devices, swapped(): return lax.ppermute(x, 'tm', [(0, 1), (1, 0)])  22.7 us
    all_to_all x2, starting transfers between devices, exchanged(): lax.all_to_all(flat, ('stn', 'tm'), split_axis=0, concat_axis=0, tiled=True)  16.3 us
    pallas_call x2, Pallas kernels, gram(): pl.pallas_call(kernel, grid_spec=pltpu.PrefetchScalarGridSpec(num_scalar_...  11.7 us
    pallas_call x3, Pallas kernels, fill(): pl.pallas_call(fill_kernel, grid_spec=pltpu.PrefetchScalarGridSpec(num_sc...  6.1 us
  transfers between devices with their start and end apart: 5, of which 4 were waited for; matrix products, arithmetic and copies ran while one was open for 0% of the time, Pallas kernels for 16%

profile of v3, /device:TPU:1, one launch (start us, length us, event | category | flops | bytes accessed | tf_op | source)
XLA Modules:
  0.0 126.3 jit_solution(18079141390813448992)
XLA Ops:
  0.0 7.2 %shard_map.73 = bf16[64,2,8,768]{3,2,1,0:T(8,128)(2,1)} custom-call(bf16[2,16,65536]{2,1,0:T(8,128)(2,1)} %x_ref.3, f32[16,4096]{1,0:T(8,128)} %taps_ref.3, bf16[64,64]{1,0:T(8,128)(2,1)} %constant.20.clone.refs_0_, f32[2,32,128]{2,1,0:T(8,128)} %constant.21.clone.refs_1_, bf16[128,256]{1,0:T(8,128)(2,1)} %constant.22.clone.refs_2_), custom_call_target="tpu_custom_call" | custom-call | flops 3000000000 | bytes 6291456 | tf_op jit(solution)/shard_map/pallas_call | solution.py:166
  7.2 11.9 %all-to-all-start = ((bf16[128,8,768]{2,1,0:T(8,128)(2,1)}), bf16[128,8,768]{2,1,0:T(8,128)(2,1)}, u32[]{:S(2)}, u32[]{:S(2)}) async-start(bf16[128,8,768]{2,1,0:T(8,128)(2,1)} %bitcast.12), calls=%async_computation | async-start | bytes 3145728 | tf_op jit(solution)/shard_map/all_to_all | solution.py:343
  19.1 15.6 %shard_map.74 = bf16[64,2,8,1280]{3,2,1,0:T(8,128)(2,1)} custom-call(bf16[2,16,65536]{2,1,0:T(8,128)(2,1)} %x_ref.3, f32[16,4096]{1,0:T(8,128)} %taps_ref.3, bf16[64,64]{1,0:T(8,128)(2,1)} %constant.20.clone.refs_0_, f32[2,32,128]{2,1,0:T(8,128)} %constant.21.clone.refs_1_, bf16[128,256]{1,0:T(8,128)(2,1)} %constant.22.clone.refs_2_), custom_call_target="tpu_custom_call" | custom-call | flops 5000000000 | bytes 10485760 | tf_op jit(solution)/shard_map/pallas_call | solution.py:166
  34.6 0.0 copy-start
  34.6 0.0 copy-start.1
  34.6 9.0 %all-to-all-done = bf16[128,8,768]{2,1,0:T(8,128)(2,1)} async-done(((bf16[128,8,768]{2,1,0:T(8,128)(2,1)}), bf16[128,8,768]{2,1,0:T(8,128)(2,1)}, u32[]{:S(2)}, u32[]{:S(2)}) %all-to-all-start) | async-done | bytes 1572896 | tf_op jit(solution)/shard_map/all_to_all | solution.py:343
  43.6 4.4 %all-to-all-start.1 = ((bf16[128,8,1280]{2,1,0:T(8,128)(2,1)}), bf16[128,8,1280]{2,1,0:T(8,128)(2,1)S(1)}, u32[]{:S(2)}, u32[]{:S(2)}) async-start(bf16[128,8,1280]{2,1,0:T(8,128)(2,1)} %bitcast.11), calls=%async_computation.1 | async-start | bytes 5242880 | tf_op jit(solution)/shard_map/all_to_all | solution.py:343
  48.1 0.0 copy-done
  48.1 0.1 copy.14
  48.2 0.1 copy.15.refs_2_.refs_3_
  48.3 0.0 copy-done.1
  48.3 0.1 pad_add_fusion.info_ref.info
  48.4 35.7 %all-to-all-done.1 = bf16[128,8,1280]{2,1,0:T(8,128)(2,1)S(1)} async-done(((bf16[128,8,1280]{2,1,0:T(8,128)(2,1)}), bf16[128,8,1280]{2,1,0:T(8,128)(2,1)S(1)}, u32[]{:S(2)}, u32[]{:S(2)}) %all-to-all-start.1) | async-done | bytes 2621472 | tf_op jit(solution)/shard_map/all_to_all | solution.py:343
  84.1 4.3 %gram.2 = (f32[2,10,2,128,256]{4,3,2,1,0:T(8,128)}, bf16[3,2,128,256]{3,2,1,0:T(8,128)(2,1)S(1)}) custom-call(s32[11]{0:T(128)S(1)} %pad_add_fusion.info_ref.info, bf16[64,2,8,768]{3,2,1,0:T(8,128)(2,1)} %bitcast.3.refs_0_.refs_1_, bf16[64,2,8,1280]{3,2,1,0:T(8,128)(2,1)S(1)} %bitcast.9, s32[4,1,256]{2,1,0:T(1,128)S(1)} %copy.15.refs_2_.refs_3_), custom_call_target="tpu_custom_call" | custom-call | flops 810000000 | bytes 2097152 | tf_op jit(solution)/shard_map/gram/pallas_call | solution.py:278
  88.4 7.4 %gram.3 = (f32[2,10,2,128,256]{4,3,2,1,0:T(8,128)}, bf16[5,2,128,256]{3,2,1,0:T(8,128)(2,1)S(1)}, bf16[2,2,128,256]{3,2,1,0:T(8,128)(2,1)S(1)}) custom-call(s32[11]{0:T(128)S(1)} %pad_add_fusion.info_ref.info, f32[2,10,2,128,256]{4,3,2,1,0:T(8,128)} %get-tuple-element.10.refs_0_, ...), custom_call_target="tpu_custom_call", output_to_operand_aliasing={{0}: (1, {})} | custom-call | flops 1890000000 | bytes 4194304 | tf_op jit(solution)/shard_map/gram/pallas_call | solution.py:278
  95.8 0.3 collective-permute-start.1
  96.1 1.2 collective-permute-start
  97.2 0.3 collective-permute-start.2
  97.5 21.8 %collective-permute-done.got_ref = bf16[3,2,128,256]{3,2,1,0:T(8,128)(2,1)S(1)} collective-permute-done((bf16[3,2,128,256]{3,2,1,0:T(8,128)(2,1)S(1)}, bf16[3,2,128,256]{3,2,1,0:T(8,128)(2,1)S(1)}, u32[]{:S(2)}, u32[]{:S(2)}) %collective-permute-start) | collective-permute-done | bytes 393248 | tf_op jit(solution)/shard_map/ppermute | solution.py:348
  119.3 2.0 %fill.3.whole_ref = f32[2,10,2,128,256]{4,3,2,1,0:T(8,128)} custom-call(s32[11]{0:T(128)S(1)} %pad_add_fusion.info_ref.info, f32[2,10,2,128,256]{4,3,2,1,0:T(8,128)} %get-tuple-element.11.whole_ref, bf16[3,2,128,256]{3,2,1,0:T(8,128)(2,1)S(1)} %collective-permute-done.got_ref), custom_call_target="tpu_custom_call", output_to_operand_aliasing={{}: (1, {})} | custom-call | flops 100000 | bytes 2359296 | tf_op jit(solution)/shard_map/fill/pallas_call | solution.py:317
  121.3 0.0 collective-permute-done.1.got_ref
  121.3 2.7 %fill.4.whole_ref = f32[2,10,2,128,256]{4,3,2,1,0:T(8,128)} custom-call(s32[11]{0:T(128)S(1)} %pad_add_fusion.info_ref.info, f32[2,10,2,128,256]{4,3,2,1,0:T(8,128)} %fill.3.whole_ref, bf16[5,2,128,256]{3,2,1,0:T(8,128)(2,1)S(1)} %collective-permute-done.1.got_ref), custom_call_target="tpu_custom_call", output_to_operand_aliasing={{}: (1, {})} | custom-call | flops 100000 | bytes 3932160 | tf_op jit(solution)/shard_map/fill/pallas_call | solution.py:317
  124.1 0.9 collective-permute-done.2.got_ref
  124.9 1.4 %fill.5 = f32[2,10,2,128,256]{4,3,2,1,0:T(8,128)} custom-call(s32[11]{0:T(128)S(1)} %pad_add_fusion.info_ref.info, f32[2,10,2,128,256]{4,3,2,1,0:T(8,128)} %fill.4.whole_ref, bf16[2,2,128,256]{3,2,1,0:T(8,128)(2,1)S(1)} %collective-permute-done.2.got_ref), custom_call_target="tpu_custom_call", output_to_operand_aliasing={{}: (1, {})} | custom-call | flops 100000 | bytes 1572864 | tf_op jit(solution)/shard_map/fill/pallas_call | solution.py:317
  (3 shorter events, 0.1 us)
Async XLA Ops:
  7.2 36.4 %all-to-all-start = ((bf16[128,8,768]{2,1,0:T(8,128)(2,1)}), bf16[128,8,768]{2,1,0:T(8,128)(2,1)}, u32[]{:S(2)}, u32[]{:S(2)}) async-start(bf16[128,8,768]{2,1,0:T(8,128)(2,1)} %bitcast.12), calls=%async_computation | async-start | bytes 3145728 | tf_op jit(solution)/shard_map/all_to_all | solution.py:343
  34.6 13.4 %copy-start = (s32[2,512]{1,0:T(2,128)S(1)}, s32[2,512]{1,0:T(2,128)}, u32[]{:S(2)}) copy-start(s32[2,512]{1,0:T(2,128)} %param.9) | copy-start | bytes 12292
  34.6 13.7 %copy-start.1 = (s32[2,10]{1,0:T(2,128)S(1)}, s32[2,10]{1,0:T(2,128)}, u32[]{:S(2)}) copy-start(s32[2,10]{1,0:T(2,128)} %param.10) | copy-start | bytes 244
  43.6 40.5 %all-to-all-start.1 = ((bf16[128,8,1280]{2,1,0:T(8,128)(2,1)}), bf16[128,8,1280]{2,1,0:T(8,128)(2,1)S(1)}, u32[]{:S(2)}, u32[]{:S(2)}) async-start(bf16[128,8,1280]{2,1,0:T(8,128)(2,1)} %bitcast.11), calls=%async_computation.1 | async-start | bytes 5242880 | tf_op jit(solution)/shard_map/all_to_all | solution.py:343
  95.8 25.6 %collective-permute-start.1 = (bf16[5,2,128,256]{3,2,1,0:T(8,128)(2,1)S(1)}, bf16[5,2,128,256]{3,2,1,0:T(8,128)(2,1)S(1)}, u32[]{:S(2)}, u32[]{:S(2)}) collective-permute-start(bf16[5,2,128,256]{3,2,1,0:T(8,128)(2,1)S(1)} %get-tuple-element.13), channel_id=1, source_target_pairs={{0,1},{1,0},{2,3},{3,2},{4,5},{5,4},{6,7},{7,6},{8,9},{9,8},{10,11... | collective-permute-start | bytes 1966088 | tf_op jit(solution)/shard_map/ppermute | solution.py:348
  96.1 23.3 %collective-permute-start = (bf16[3,2,128,256]{3,2,1,0:T(8,128)(2,1)S(1)}, bf16[3,2,128,256]{3,2,1,0:T(8,128)(2,1)S(1)}, u32[]{:S(2)}, u32[]{:S(2)}) collective-permute-start(bf16[3,2,128,256]{3,2,1,0:T(8,128)(2,1)S(1)} %get-tuple-element.12), channel_id=1, source_target_pairs={{0,1},{1,0},{2,3},{3,2},{4,5},{5,4},{6,7},{7,6},{8,9},{9,8},{10,11... | collective-permute-start | bytes 1179656 | tf_op jit(solution)/shard_map/ppermute | solution.py:348
  97.2 27.7 %collective-permute-start.2 = (bf16[2,2,128,256]{3,2,1,0:T(8,128)(2,1)S(1)}, bf16[2,2,128,256]{3,2,1,0:T(8,128)(2,1)S(1)}, u32[]{:S(2)}, u32[]{:S(2)}) collective-permute-start(bf16[2,2,128,256]{3,2,1,0:T(8,128)(2,1)S(1)} %get-tuple-element.14), channel_id=1, source_target_pairs={{0,1},{1,0},{2,3},{3,2},{4,5},{5,4},{6,7},{7,6},{8,9},{9,8},{10,11... | collective-permute-start | bytes 786440 | tf_op jit(solution)/shard_map/ppermute | solution.py:348
